TPU v7x, 32 devices: a whole 2x2x4 slice. The times are simulated.
32 devices in a mesh: row: 4 (over x, core), col: 8 (over z, y).
Axes of the slice: x: 2, y: 2, z: 4, core: 2. Of those that a mesh axis runs over, the one named last changes fastest.
Arguments:
- eigvecs: float32 [1024, 1024], P('row', 'col'), may hold values from -6 to 6
- offsets: int32 [1], replicated, may hold values from 0 to 127
- plan: int32 [1, 6], replicated, may hold values from 0 to 7
- refl_v: float32 [8, 255, 128], P('col')
- refl_t: float32 [8, 128, 128], P('col'), as said below
Outputs:
- updated: float32 [1024, 1024], P('row', 'col')
Inputs may be any that keep to these rules, and one draw needn't show every extreme that they name: For each bank entry, I - refl_v refl_t refl_v^T is orthogonal up to rounding.
All inputs are finite; a program needn't handle non-finite values.
Results may differ from a plain program's by a relative error of at most 0.00015.
Values sent between devices are 32-bit elements; how exact they have to be, the bound alone decides.
No kernel may reach another device: no remote copies, remote signals or barrier semaphores. Data moves between devices by JAX's collectives and lax.ppermute only.
A program may use at most 64 MiB of HBM per device.

v0:
```python
import functools

import jax
import jax.numpy as jnp
from jax import lax
from jax.experimental import pallas as pl
from jax.experimental.pallas import tpu as pltpu
from jax.sharding import PartitionSpec as P


AXES = ("row", "col")
F32, BF16 = jnp.float32, jnp.bfloat16
NT = (((1,), (1,)), ((), ()))


def iotas(rows, cols):
    return lax.broadcasted_iota(jnp.int32, (rows, cols), 0), lax.broadcasted_iota(jnp.int32, (rows, cols), 1)


def pack_kernel(both_any, wire_ref, both_ref, sem):
    nb = wire_ref.shape[1]
    half = nb // 2
    copy = pltpu.make_async_copy(both_any.at[:, 0, :], both_ref.at[0 : 3 * nb - 1], sem)
    copy.start()
    copy.wait()
    row, col = iotas(nb, nb)
    factor = both_ref[0:nb, :]
    low = both_ref[nb : 2 * nb, :]
    up = pltpu.roll(both_ref[2 * nb - 1 : 3 * nb - 1, :], nb - 1, axis=0)
    wire_ref[0:nb, :] = jnp.where(row > col, low, jnp.where(row < col, up, factor))
    turned = jnp.transpose(jnp.concatenate([factor[half:, :], factor[:half, :]], axis=0))[half:, :]
    row, col = iotas(half, nb)
    wire_ref[nb:, :] = jnp.where(row < col, factor[:half, :], turned)


def pack(vectors, factor):
    nb = factor.shape[2]
    both = jnp.concatenate([factor.reshape(nb, 1, nb), jnp.transpose(vectors, (1, 0, 2))], axis=0)
    return pl.pallas_call(
        pack_kernel,
        out_shape=jax.ShapeDtypeStruct((nb + nb // 2, nb), F32),
        in_specs=[pl.BlockSpec(memory_space=pl.ANY)],
        out_specs=pl.BlockSpec(memory_space=pltpu.VMEM),
        scratch_shapes=[pltpu.VMEM((3 * nb, nb), F32), pltpu.SemaphoreType.DMA],
        compiler_params=pltpu.CompilerParams(vmem_limit_bytes=4 * 2**20),
        name="pack",
    )(both)


def split(x):
    high = x.astype(BF16)
    return high, (x - high.astype(F32)).astype(BF16)


def dot(a, b, dims=(((1,), (0,)), ((), ()))):
    return lax.dot_general(a, b, dims, preferred_element_type=F32)


def dot3(a, b, dims=(((1,), (0,)), ((), ()))):
    return dot(a[0], b[0], dims) + (dot(a[1], b[0], dims) + dot(a[0], b[1], dims))


def unpack(packed):
    nb = packed.shape[1]
    half = nb // 2
    row, col = iotas(nb, nb)
    row_h, col_h = iotas(half, nb)
    diagonal = row == col
    square, tail = packed[:nb], packed[nb:]
    low = split(jnp.where(row > col, square, diagonal.astype(F32)))
    up = split(jnp.where(row < col, square, 0.0))
    below = jnp.where(row_h > col_h, tail, 0.0)
    turned = jnp.transpose(jnp.concatenate([jnp.zeros_like(below), below], axis=0))[:half, :]
    factor = jnp.concatenate([jnp.where(row_h < col_h, tail, 0.0), turned], axis=0)
    factor = split(jnp.where(diagonal, square, factor))
    return low + up + split(dot3(factor, low, NT)) + split(dot3(factor, up, NT))


def unpack_into(pieces_ref, banks, slots, n_col):
    odd = lax.rem(lax.axis_index("row"), 2)
    my_col = lax.axis_index("col")
    for bank, slot in zip(banks, slots):
        entry = jnp.bitwise_xor(my_col, slot_distance(slot, n_col, odd))
        for i, piece in enumerate(unpack(bank[...])):
            pieces_ref[entry, i] = piece


def near_kernel(n_col, slots, *refs):
    unpack_into(refs[-1], refs[:-1], slots, n_col)


def apply_kernel(n_col, n_row, n_blocks, slots, *refs):
    table_any, refs = refs[0], refs[1:]
    banks, refs = refs[: len(slots)], refs[len(slots) :]
    parts, refs = refs[:n_row], refs[n_row:]
    _, out_any, pieces_ref, rows_ref, solved_ref, plan_ref, sems = refs
    nb = banks[0].shape[1]
    own_rows, own_cols = parts[0].shape
    my_row = lax.axis_index("row")
    table = pltpu.make_async_copy(table_any, plan_ref, sems.at[0])
    table.start()

    for step in range(n_row):
        start = pl.multiple_of(jnp.bitwise_xor(my_row, step) * own_rows + nb, nb)
        rows_ref[pl.ds(start, own_rows), :] = parts[step][...]
    unpack_into(pieces_ref, banks, slots, n_col)

    zero = jnp.zeros((nb, own_cols), BF16)
    for index in (0, 1, n_blocks + 2, n_blocks + 3):
        for i in range(2):
            solved_ref[index, i] = zero
    table.wait()
    first = plan_ref[0, n_blocks]

    def low_of(entry):
        return pieces_ref[entry, 0], pieces_ref[entry, 1]

    def up_of(entry):
        return pieces_ref[entry, 2], pieces_ref[entry, 3]

    def block(index):
        entry = plan_ref[0, index]
        before = plan_ref[0, jnp.maximum(index - 1, 0)]
        window = split(rows_ref[pl.ds(first + (index + 1) * nb, 2 * nb), :])
        lead_low = pieces_ref[entry, 4], pieces_ref[entry, 5]
        lead = [jnp.concatenate([lead_low[i], pieces_ref[entry, 6 + i]], axis=1) for i in range(2)]
        free = dot3(lead, window)
        link = split(dot3(lead_low, up_of(before)))
        return free, link

    def store(index, value):
        value = split(value)
        for i in range(2):
            solved_ref[index + 2, i] = value[i]
        return value

    def solved_of(index):
        return solved_ref[index + 2, 0], solved_ref[index + 2, 1]

    if n_blocks <= 8:
        work = [block(index) for index in range(n_blocks)]
        last = store(0, work[0][0])
        for index in range(1, n_blocks):
            free, link = work[index]
            last = store(index, free - dot3(link, last))
    else:
        store(0, block(0)[0])

        def step(index, carry):
            free, link = block(index)
            store(index, free - dot3(link, solved_of(index - 1)))
            return carry

        lax.fori_loop(1, n_blocks, step, 0)

    mine = my_row * own_rows
    tile = lax.div(mine - first + nb, nb) - 1
    copies = []
    for k in range(own_rows // nb + 1):
        t = jnp.minimum(tile + k, n_blocks + 1)
        low_entry = plan_ref[0, jnp.clip(t, 0, n_blocks - 1)]
        up_entry = plan_ref[0, jnp.clip(t - 1, 0, n_blocks - 1)]
        window = pl.ds(first + (t + 1) * nb, nb)
        moved = dot3(up_of(up_entry), solved_of(t - 1)) + dot3(low_of(low_entry), solved_of(t))
        rows_ref[window, :] = rows_ref[window, :] - moved
        if k > 0:
            source = pl.ds(pl.multiple_of(mine + k * nb, nb), nb)
            copy = pltpu.make_async_copy(
                rows_ref.at[source, :], out_any.at[pl.ds((k - 1) * nb, nb), :], sems.at[k]
            )
            copy.start()
            copies.append(copy)
    for copy in copies:
        copy.wait()


def slot_distance(slot, n_col, odd):
    pairs = n_col // 2
    if slot == 0:
        return jnp.int32(0)
    step = (slot - 1) % pairs
    even_distance, odd_distance = n_col - 1 - 2 * step, n_col - 2 - 2 * step
    if step == pairs - 1:
        return jnp.int32(1)
    if slot > pairs:
        even_distance, odd_distance = odd_distance, even_distance
    return even_distance + odd * (odd_distance - even_distance)


def on_device(eigvecs, offsets, plan, refl_v, refl_t):
    n_row, n_col = lax.axis_size("row"), lax.axis_size("col")
    own_rows, own_cols = eigvecs.shape
    nb = refl_t.shape[2]
    n_blocks = plan.shape[1]
    pairs = n_col // 2

    def send(x, row_by, col_by):
        to = [
            (r * n_col + c, (r ^ row_by) * n_col + (c ^ col_by[r % 2]))
            for r in range(n_row)
            for c in range(n_col)
        ]
        return lax.ppermute(x, AXES, to)

    wire = pack(refl_v, refl_t)
    got = []
    for step in range(pairs):
        by = (n_col - 1 - 2 * step, n_col - 2 - 2 * step)
        if step == pairs - 1:
            by = (1, 1)
        got.append(send(wire, 0, by))
    parts = {0: eigvecs}
    for step in range(2, n_row, 2):
        parts[step] = send(eigvecs, step, (0, 0))
    swaps = [send(x, 1, (0, 0)) for x in got[:-1]]
    for step in range(0, n_row, 2):
        parts[step + 1] = send(parts[step], 1, (0, 0))
    parts = [parts[step] for step in range(n_row)]
    banks = [wire] + got + swaps

    table = jnp.pad(plan, ((0, 7), (0, nb - n_blocks)), constant_values=offsets[0])
    far = list(range(pairs + 1, n_col))
    near = [slot for slot in range(n_col) if slot not in far]
    vmem = pl.BlockSpec(memory_space=pltpu.VMEM)
    here = pl.BlockSpec(memory_space=pl.ANY)
    pieces = jax.ShapeDtypeStruct((n_col, 8, nb, nb), BF16)
    limit = pltpu.CompilerParams(vmem_limit_bytes=max(12 * 2**20, 8 * n_blocks * 2**17))
    pieces = pl.pallas_call(
        functools.partial(near_kernel, n_col, near),
        out_shape=pieces,
        in_specs=[vmem] * len(near),
        out_specs=vmem,
        compiler_params=limit,
        name="near_entries",
    )(*[banks[slot] for slot in near])
    n_in = 1 + len(far) + n_row
    return pl.pallas_call(
        functools.partial(apply_kernel, n_col, n_row, n_blocks, far),
        out_shape=(jax.ShapeDtypeStruct((own_rows, own_cols), F32), pieces),
        in_specs=[here] + [vmem] * (len(far) + n_row + 1),
        out_specs=(here, vmem),
        scratch_shapes=[
            pltpu.VMEM((n_row * own_rows + 3 * nb, own_cols), F32),
            pltpu.VMEM((n_blocks + 4, 2, nb, own_cols), BF16),
            pltpu.SMEM((8, nb), jnp.int32),
            pltpu.SemaphoreType.DMA((1 + own_rows // nb,)),
        ],
        input_output_aliases={n_in: 1},
        compiler_params=limit,
        name="apply_blocks",
    )(table, *[banks[slot] for slot in far], *parts, pieces)[0]


def solution(mesh):
    in_specs = (P("row", "col"), P(), P(), P("col", None, None), P("col", None, None))
    return jax.shard_map(
        on_device, mesh=mesh, in_specs=in_specs, out_specs=P("row", "col"), check_vma=False
    )
```

profile of v0, /device:TPU:0, one launch (start us, length us, event | category | flops | bytes accessed | tf_op | source)
XLA Modules:
  0.0 24.0 jit_solution(3014998594559785551)
XLA Ops:
  0.0 0.0 copy-start
  0.0 3.0 %collective-permute-start.7 = (f32[256,128]{1,0:T(8,128)}, f32[256,128]{1,0:T(8,128)S(1)}, u32[]{:S(2)}, u32[]{:S(2)}) collective-permute-start(f32[256,128]{1,0:T(8,128)} %refs_4_.1), channel_id=1, source_target_pairs={{0,16},{1,17},{2,18},{3,19},{4,20},{5,21},{6,22},{7,23},{8,24},{9,... | collective-permute-start | bytes 393224 | tf_op jit(solution)/shard_map/ppermute | solution.py:203
  3.0 1.1 %pad_maximum_fusion.both_any = f32[383,1,128]{2,1,0:T(1,128)S(1)} fusion(f32[255,1,128]{2,1,0:T(1,128)} %bitcast.4, f32[128,1,128]{2,1,0:T(1,128)} %bitcast.5), kind=kLoop, calls=%fused_computation | loop fusion | flops 49024 | bytes 392192 | tf_op jit(solution)/shard_map/concatenate | solution.py:38
  4.0 0.4 %pack.1.refs_0_ = f32[192,128]{1,0:T(8,128)S(1)} custom-call(f32[383,1,128]{2,1,0:T(1,128)S(1)} %pad_maximum_fusion.both_any), custom_call_target="tpu_custom_call" | custom-call | tf_op jit(solution)/shard_map/pack/pallas_call | solution.py:39
  4.4 1.6 %collective-permute-start.9 = (f32[192,128]{1,0:T(8,128)S(1)}, f32[192,128]{1,0:T(8,128)S(1)}, u32[]{:S(2)}, u32[]{:S(2)}) collective-permute-start(f32[192,128]{1,0:T(8,128)S(1)} %pack.1.refs_0_), channel_id=1, source_target_pairs={{0,1},{1,0},{2,3},{3,2},{4,5},{5,4},{6,7},{7,6},{8,9},{9,8},{10,11... | collective-permute-start | bytes 294920 | tf_op jit(solution)/shard_map/ppermute | solution.py:203
  6.0 1.5 %collective-permute-start.4 = (f32[192,128]{1,0:T(8,128)S(1)}, f32[192,128]{1,0:T(8,128)S(1)}, u32[]{:S(2)}, u32[]{:S(2)}) collective-permute-start(f32[192,128]{1,0:T(8,128)S(1)} %pack.1.refs_0_), channel_id=1, source_target_pairs={{0,3},{1,2},{2,1},{3,0},{4,7},{5,6},{6,5},{7,4},{8,10},{9,11},{10,... | collective-permute-start | bytes 294920 | tf_op jit(solution)/shard_map/ppermute | solution.py:203
  7.5 3.5 %collective-permute-start.2 = (f32[192,128]{1,0:T(8,128)S(1)}, f32[192,128]{1,0:T(8,128)S(1)}, u32[]{:S(2)}, u32[]{:S(2)}) collective-permute-start(f32[192,128]{1,0:T(8,128)S(1)} %pack.1.refs_0_), channel_id=1, source_target_pairs={{0,5},{1,4},{2,7},{3,6},{4,1},{5,0},{6,3},{7,2},{8,12},{9,13},{10,... | collective-permute-start | bytes 294920 | tf_op jit(solution)/shard_map/ppermute | solution.py:203
  11.1 0.2 collective-permute-start
  11.2 0.0 collective-permute-done.9.refs_4_
  11.2 0.0 collective-permute-start.6
  11.2 0.0 collective-permute-done.7.refs_6_
  11.2 0.5 %collective-permute-start.8 = (f32[256,128]{1,0:T(8,128)S(1)}, f32[256,128]{1,0:T(8,128)S(1)}, u32[]{:S(2)}, u32[]{:S(2)}) collective-permute-start(f32[256,128]{1,0:T(8,128)S(1)} %collective-permute-done.7.refs_6_), channel_id=1, source_target_pairs={{0,8},{1,9},{2,10},{3,11},{4,12},{5,13},{6,14},{7,15},{8,0},{9,1},... | collective-permute-start | bytes 393224 | tf_op jit(solution)/shard_map/ppermute | solution.py:203
  11.8 0.3 %collective-permute-done.4.refs_3_ = f32[192,128]{1,0:T(8,128)S(1)} collective-permute-done((f32[192,128]{1,0:T(8,128)S(1)}, f32[192,128]{1,0:T(8,128)S(1)}, u32[]{:S(2)}, u32[]{:S(2)}) %collective-permute-start.4) | collective-permute-done | bytes 98336 | tf_op jit(solution)/shard_map/ppermute | solution.py:203
  12.0 0.0 collective-permute-start.5
  12.0 4.3 %collective-permute-done.2.refs_2_ = f32[192,128]{1,0:T(8,128)S(1)} collective-permute-done((f32[192,128]{1,0:T(8,128)S(1)}, f32[192,128]{1,0:T(8,128)S(1)}, u32[]{:S(2)}, u32[]{:S(2)}) %collective-permute-start.2) | collective-permute-done | bytes 98336 | tf_op jit(solution)/shard_map/ppermute | solution.py:203
  16.3 0.0 collective-permute-start.3
  16.3 2.1 %collective-permute-done.refs_1_ = f32[192,128]{1,0:T(8,128)S(1)} collective-permute-done((f32[192,128]{1,0:T(8,128)S(1)}, f32[192,128]{1,0:T(8,128)S(1)}, u32[]{:S(2)}, u32[]{:S(2)}) %collective-permute-start) | collective-permute-done | bytes 98336 | tf_op jit(solution)/shard_map/ppermute | solution.py:203
  18.4 0.0 collective-permute-start.1
  19.1 0.7 %pad.4.refs_0_ = s32[8,128]{1,0:T(8,128)S(1)} pad(s32[1,6]{1,0:T(1,128)} %param.7, s32[]{:T(128)} %bitcast.3), padding=0_7x0_122 | pad | bytes 4124 | tf_op jit(solution)/shard_map/jit(_pad)/pad | solution.py:221
  19.8 0.8 %near_entries.1.refs_8_ = bf16[8,8,128,128]{3,2,1,0:T(8,128)(2,1)S(1)} custom-call(f32[192,128]{1,0:T(8,128)S(1)} %pack.1.refs_0_, f32[192,128]{1,0:T(8,128)S(1)} %collective-permute-done.refs_1_, f32[192,128]{1,0:T(8,128)S(1)} %collective-permute-done.2.refs_2_, f32[192,128]{1,0:T(8,128)S(1)} %collective-permute-done.4.refs_3_, ...), custom_call_target="tpu_custom_call" | custom-call | tf_op jit(solution)/shard_map/near_entries/pallas_call | solution.py:228
  20.6 0.0 collective-permute-done.6.refs_5_
  20.6 0.0 collective-permute-done.5.refs_3_
  20.6 0.0 collective-permute-done.3.refs_2_
  20.6 0.0 collective-permute-done.1.refs_1_
  20.6 0.0 collective-permute-done.8.refs_7_
  20.6 0.0 copy-done
  20.6 3.3 %apply_blocks.1 = (f32[256,128]{1,0:T(8,128)}, bf16[8,8,128,128]{3,2,1,0:T(8,128)(2,1)S(1)}) custom-call(s32[8,128]{1,0:T(8,128)S(1)} %pad.4.refs_0_, f32[192,128]{1,0:T(8,128)S(1)} %collective-permute-done.1.refs_1_, f32[192,128]{1,0:T(8,128)S(1)} %collective-permute-done.3.refs_2_, ...), custom_call_target="tpu_custom_call", output_to_operand_aliasing={{1}: (8, {})} | custom-call | tf_op jit(solution)/shard_map/apply_blocks/pallas_call | solution.py:237
Async XLA Ops:
  0.0 20.6 %copy-start = (f32[256,128]{1,0:T(8,128)S(1)}, f32[256,128]{1,0:T(8,128)}, u32[]{:S(2)}) copy-start(f32[256,128]{1,0:T(8,128)} %refs_4_.1) | copy-start | bytes 393220
  0.0 11.2 %collective-permute-start.7 = (f32[256,128]{1,0:T(8,128)}, f32[256,128]{1,0:T(8,128)S(1)}, u32[]{:S(2)}, u32[]{:S(2)}) collective-permute-start(f32[256,128]{1,0:T(8,128)} %refs_4_.1), channel_id=1, source_target_pairs={{0,16},{1,17},{2,18},{3,19},{4,20},{5,21},{6,22},{7,23},{8,24},{9,... | collective-permute-start | bytes 393224 | tf_op jit(solution)/shard_map/ppermute | solution.py:203
  4.4 6.8 %collective-permute-start.9 = (f32[192,128]{1,0:T(8,128)S(1)}, f32[192,128]{1,0:T(8,128)S(1)}, u32[]{:S(2)}, u32[]{:S(2)}) collective-permute-start(f32[192,128]{1,0:T(8,128)S(1)} %pack.1.refs_0_), channel_id=1, source_target_pairs={{0,1},{1,0},{2,3},{3,2},{4,5},{5,4},{6,7},{7,6},{8,9},{9,8},{10,11... | collective-permute-start | bytes 294920 | tf_op jit(solution)/shard_map/ppermute | solution.py:203
  6.0 6.0 %collective-permute-start.4 = (f32[192,128]{1,0:T(8,128)S(1)}, f32[192,128]{1,0:T(8,128)S(1)}, u32[]{:S(2)}, u32[]{:S(2)}) collective-permute-start(f32[192,128]{1,0:T(8,128)S(1)} %pack.1.refs_0_), channel_id=1, source_target_pairs={{0,3},{1,2},{2,1},{3,0},{4,7},{5,6},{6,5},{7,4},{8,10},{9,11},{10,... | collective-permute-start | bytes 294920 | tf_op jit(solution)/shard_map/ppermute | solution.py:203
  7.5 8.8 %collective-permute-start.2 = (f32[192,128]{1,0:T(8,128)S(1)}, f32[192,128]{1,0:T(8,128)S(1)}, u32[]{:S(2)}, u32[]{:S(2)}) collective-permute-start(f32[192,128]{1,0:T(8,128)S(1)} %pack.1.refs_0_), channel_id=1, source_target_pairs={{0,5},{1,4},{2,7},{3,6},{4,1},{5,0},{6,3},{7,2},{8,12},{9,13},{10,... | collective-permute-start | bytes 294920 | tf_op jit(solution)/shard_map/ppermute | solution.py:203
  11.1 7.4 %collective-permute-start = (f32[192,128]{1,0:T(8,128)S(1)}, f32[192,128]{1,0:T(8,128)S(1)}, u32[]{:S(2)}, u32[]{:S(2)}) collective-permute-start(f32[192,128]{1,0:T(8,128)S(1)} %pack.1.refs_0_), channel_id=1, source_target_pairs={{0,7},{1,6},{2,5},{3,4},{4,3},{5,2},{6,1},{7,0},{8,14},{9,15},{10,... | collective-permute-start | bytes 294920 | tf_op jit(solution)/shard_map/ppermute | solution.py:203
  11.2 9.4 %collective-permute-start.6 = (f32[256,128]{1,0:T(8,128)}, f32[256,128]{1,0:T(8,128)S(1)}, u32[]{:S(2)}, u32[]{:S(2)}) collective-permute-start(f32[256,128]{1,0:T(8,128)} %refs_4_.1), channel_id=1, source_target_pairs={{0,8},{1,9},{2,10},{3,11},{4,12},{5,13},{6,14},{7,15},{8,0},{9,1},... | collective-permute-start | bytes 393224 | tf_op jit(solution)/shard_map/ppermute | solution.py:203
  11.2 9.4 %collective-permute-start.8 = (f32[256,128]{1,0:T(8,128)S(1)}, f32[256,128]{1,0:T(8,128)S(1)}, u32[]{:S(2)}, u32[]{:S(2)}) collective-permute-start(f32[256,128]{1,0:T(8,128)S(1)} %collective-permute-done.7.refs_6_), channel_id=1, source_target_pairs={{0,8},{1,9},{2,10},{3,11},{4,12},{5,13},{6,14},{7,15},{8,0},{9,1},... | collective-permute-start | bytes 393224 | tf_op jit(solution)/shard_map/ppermute | solution.py:203
  12.0 8.6 %collective-permute-start.5 = (f32[192,128]{1,0:T(8,128)S(1)}, f32[192,128]{1,0:T(8,128)S(1)}, u32[]{:S(2)}, u32[]{:S(2)}) collective-permute-start(f32[192,128]{1,0:T(8,128)S(1)} %collective-permute-done.4.refs_3_), channel_id=1, source_target_pairs={{0,8},{1,9},{2,10},{3,11},{4,12},{5,13},{6,14},{7,15},{8,0},{9,1},... | collective-permute-start | bytes 294920 | tf_op jit(solution)/shard_map/ppermute | solution.py:203
  16.3 4.3 %collective-permute-start.3 = (f32[192,128]{1,0:T(8,128)S(1)}, f32[192,128]{1,0:T(8,128)S(1)}, u32[]{:S(2)}, u32[]{:S(2)}) collective-permute-start(f32[192,128]{1,0:T(8,128)S(1)} %collective-permute-done.2.refs_2_), channel_id=1, source_target_pairs={{0,8},{1,9},{2,10},{3,11},{4,12},{5,13},{6,14},{7,15},{8,0},{9,1},... | collective-permute-start | bytes 294920 | tf_op jit(solution)/shard_map/ppermute | solution.py:203
  18.4 2.2 %collective-permute-start.1 = (f32[192,128]{1,0:T(8,128)S(1)}, f32[192,128]{1,0:T(8,128)S(1)}, u32[]{:S(2)}, u32[]{:S(2)}) collective-permute-start(f32[192,128]{1,0:T(8,128)S(1)} %collective-permute-done.refs_1_), channel_id=1, source_target_pairs={{0,8},{1,9},{2,10},{3,11},{4,12},{5,13},{6,14},{7,15},{8,0},{9,1},... | collective-permute-start | bytes 294920 | tf_op jit(solution)/shard_map/ppermute | solution.py:203
where the time goes:
time: 24.2 us; the launch traced here: 24 us
  starting transfers between devices  10.3 us (43%)
  waiting for transfers between devices  6.7 us (28%)
  Pallas kernels  4.53 us (19%)
  other arithmetic  1.08 us (4%)
  between operations  0.73 us (3%)
  local copies, waits for them, and re-layouts  0.67 us (3%)
    ppermute x10, starting transfers between devices, send(): return lax.ppermute(x, AXES, to)  10.3 us
    ppermute x10, waiting for transfers between devices, send(): return lax.ppermute(x, AXES, to)  6.7 us
    pallas_call x1, Pallas kernels, on_device(): pl.pallas_call(functools.partial(apply_kernel, n_col, n_row, n_blocks, fa...  3.34 us
    concatenate x1, other arithmetic, pack(): jnp.concatenate([factor.reshape(nb, 1, nb), jnp.transpose(vectors, (1, 0,...  1.08 us
    pallas_call x1, Pallas kernels, on_device(): pl.pallas_call(functools.partial(near_kernel, n_col, near), out_shape=pie...  0.82 us
    pad x1, local copies, waits for them, and re-layouts, on_device(): jnp.pad(plan, ((0, 7), (0, nb - n_blocks)), constant_values=offsets[0])  0.66 us
  transfers between devices with their start and end apart: 10, of which 3 were waited for; matrix products, arithmetic and copies ran while one was open for 7% of the time, Pallas kernels for 5%

commit v1 on v0

v1 whole, which is shorter than its diff:
```python
import functools

import jax
import jax.numpy as jnp
from jax import lax
from jax.experimental import pallas as pl
from jax.experimental.pallas import tpu as pltpu
from jax.sharding import PartitionSpec as P


AXES = ("row", "col")
F32, BF16 = jnp.float32, jnp.bfloat16


def iotas(rows, cols):
    return lax.broadcasted_iota(jnp.int32, (rows, cols), 0), lax.broadcasted_iota(jnp.int32, (rows, cols), 1)


def pack_kernel(both_any, wire_ref, both_ref, sem):
    nb = wire_ref.shape[1]
    half, quarter = nb // 2, nb // 4
    copy = pltpu.make_async_copy(both_any.at[:, 0, :], both_ref.at[0 : 3 * nb - 1], sem)
    copy.start()
    copy.wait()
    row, col = iotas(nb, nb)
    factor = both_ref[0:nb, :]
    low = both_ref[nb : 2 * nb, :]
    up = pltpu.roll(both_ref[2 * nb - 1 : 3 * nb - 1, :], nb - 1, axis=0)
    wire_ref[0:nb, :] = jnp.where(row > col, low, jnp.where(row < col, up, factor))
    turned = jnp.transpose(jnp.concatenate([factor[half:, :], factor[:half, :]], axis=0))[half:, :]
    row, col = iotas(half, nb)
    square = jnp.where(row < col, factor[:half, :], turned)
    _, col = iotas(quarter, nb)
    wire_ref[nb:, :] = jnp.where(col < half, square[:quarter], pltpu.roll(square[quarter:], half, axis=1))


def pack(vectors, factor):
    nb = factor.shape[2]
    both = jnp.concatenate([factor.reshape(nb, 1, nb), jnp.transpose(vectors, (1, 0, 2))], axis=0)
    return pl.pallas_call(
        pack_kernel,
        out_shape=jax.ShapeDtypeStruct((nb + nb // 4, nb), F32),
        in_specs=[pl.BlockSpec(memory_space=pl.ANY)],
        out_specs=pl.BlockSpec(memory_space=pltpu.VMEM),
        scratch_shapes=[pltpu.VMEM((3 * nb, nb), F32), pltpu.SemaphoreType.DMA],
        compiler_params=pltpu.CompilerParams(vmem_limit_bytes=4 * 2**20),
        name="pack",
    )(both)


def split(x):
    high = x.astype(BF16)
    return high, (x - high.astype(F32)).astype(BF16)


def dot(a, b):
    return jnp.dot(a, b, preferred_element_type=F32)


def dot3(a, b):
    return dot(a[0], b[0]) + (dot(a[1], b[0]) + dot(a[0], b[1]))


def twice(pair):
    return [jnp.concatenate([x, x], axis=0) for x in pair]


def unpack_into(pieces_ref, banks, distances):
    for i in range(0, len(banks), 8):
        unpack_together(pieces_ref, banks[i : i + 8], distances[i : i + 8])


def unpack_together(pieces_ref, banks, distances):
    nb = banks[0].shape[1]
    half = nb // 2
    row, col = iotas(nb, nb)
    row_h, col_h = iotas(half, nb)
    unit = (row == col).astype(F32)
    odd = lax.rem(lax.axis_index("row"), 2)
    my_col = lax.axis_index("col")
    entries = [jnp.bitwise_xor(my_col, even_by + odd * (odd_by - even_by)) for even_by, odd_by in distances]

    across, whole, first, last = [], [], [], []
    for bank, entry in zip(banks, entries):
        square, tail = bank[0:nb, :], bank[nb:, :]
        low = split(jnp.where(row > col, square, unit))
        up = split(jnp.where(row < col, square, 0.0))
        for i in range(2):
            pieces_ref[entry, i] = low[i]
            pieces_ref[entry, 2 + i] = up[i]
        whole.append([jnp.concatenate([low[i], up[i]], axis=0) for i in range(2)])
        turned = jnp.transpose(square)
        turned = [jnp.where(row < col, turned, unit), jnp.where(row > col, turned, 0.0)]
        across.append(jnp.concatenate(turned, axis=1))
        tail = jnp.concatenate([tail, pltpu.roll(tail, half, axis=1)], axis=0)
        below = jnp.where(row_h > col_h, tail, 0.0)
        below = jnp.transpose(jnp.concatenate([jnp.zeros_like(below), below], axis=0))[:half, :]
        above = jnp.where((row_h < col_h) & (col_h < half), tail, 0.0)
        first.append(split(jnp.where(row_h == col_h, square[:half], above)))
        last.append(split(jnp.where(row_h + half == col_h, square[half:], below)))
    split_across = [split(x) for x in across]
    lead_last = [split(dot3(x, y)) for x, y in zip(last, split_across)]
    beside = [dot3([x[:half] for x in y], z) for y, z in zip(split_across, whole)]
    beside = [split(jnp.where(col_h < half, 0.0, x)) for x in beside]
    rest = [split(x[:half] - dot3(y, twice(z))) for x, y, z in zip(across, beside, lead_last)]
    lead_first = [split(dot3(x, twice(y))) for x, y in zip(first, rest)]
    for entry, top, bottom in zip(entries, lead_first, lead_last):
        for i in range(2):
            for part in range(2):
                lanes = slice(part * nb, (part + 1) * nb)
                pieces_ref[entry, 4 + 2 * part + i, 0:half] = top[i][:, lanes]
                pieces_ref[entry, 4 + 2 * part + i, half:nb] = bottom[i][:, lanes]


def unpack_kernel(distances, *refs):
    unpack_into(refs[-1], refs[: len(distances)], distances)


def apply_kernel(distances, n_row, n_blocks, *refs):
    table_any, refs = refs[0], refs[1:]
    banks, refs = refs[: len(distances)], refs[len(distances) :]
    parts, refs = refs[:n_row], refs[n_row:]
    _, out_any, pieces_ref, rows_ref, solved_ref, plan_ref, sems = refs
    nb = pieces_ref.shape[2]
    own_rows, own_cols = parts[0].shape
    my_row = lax.axis_index("row")
    table = pltpu.make_async_copy(table_any, plan_ref, sems.at[0])
    table.start()

    for step in range(n_row):
        start = pl.multiple_of(jnp.bitwise_xor(my_row, step) * own_rows + nb, nb)
        rows_ref[pl.ds(start, own_rows), :] = parts[step][...]
    unpack_into(pieces_ref, banks, distances)

    zero = jnp.zeros((nb, own_cols), BF16)
    for index in (0, 1, n_blocks + 2, n_blocks + 3):
        for i in range(2):
            solved_ref[index, i] = zero
    table.wait()
    first = plan_ref[0, n_blocks]

    def low_of(entry):
        return pieces_ref[entry, 0], pieces_ref[entry, 1]

    def up_of(entry):
        return pieces_ref[entry, 2], pieces_ref[entry, 3]

    def block(index):
        entry = plan_ref[0, index]
        before = plan_ref[0, jnp.maximum(index - 1, 0)]
        window = split(rows_ref[pl.ds(first + (index + 1) * nb, 2 * nb), :])
        lead_low = pieces_ref[entry, 4], pieces_ref[entry, 5]
        lead = [jnp.concatenate([lead_low[i], pieces_ref[entry, 6 + i]], axis=1) for i in range(2)]
        free = dot3(lead, window)
        link = split(dot3(lead_low, up_of(before)))
        return free, link

    def store(index, value):
        value = split(value)
        for i in range(2):
            solved_ref[index + 2, i] = value[i]
        return value

    def solved_of(index):
        return solved_ref[index + 2, 0], solved_ref[index + 2, 1]

    if n_blocks <= 8:
        work = [block(index) for index in range(n_blocks)]
        last = store(0, work[0][0])
        odd = last
        for index in range(1, n_blocks, 2):
            before, (free, link) = work[index - 1], work[index]
            joined = free - dot3(link, last if index == 1 else split(before[0]))
            if index == 1:
                odd = store(index, joined)
                continue
            both = split(dot3(link, before[1]))
            store(index - 1, before[0] - dot3(before[1], odd))
            odd = store(index, joined + dot3(both, odd))
        if n_blocks % 2 and n_blocks > 1:
            free, link = work[-1]
            store(n_blocks - 1, free - dot3(link, odd))
    else:
        store(0, block(0)[0])

        def step(index, carry):
            free, link = block(index)
            store(index, free - dot3(link, solved_of(index - 1)))
            return carry

        lax.fori_loop(1, n_blocks, step, 0)

    mine = my_row * own_rows
    tile = lax.div(mine - first + nb, nb) - 1
    copies = []
    for k in range(own_rows // nb + 1):
        t = jnp.minimum(tile + k, n_blocks + 1)
        low_entry = plan_ref[0, jnp.clip(t, 0, n_blocks - 1)]
        up_entry = plan_ref[0, jnp.clip(t - 1, 0, n_blocks - 1)]
        window = pl.ds(first + (t + 1) * nb, nb)
        moved = dot3(up_of(up_entry), solved_of(t - 1)) + dot3(low_of(low_entry), solved_of(t))
        rows_ref[window, :] = rows_ref[window, :] - moved
        if k > 0:
            source = pl.ds(pl.multiple_of(mine + k * nb, nb), nb)
            copy = pltpu.make_async_copy(
                rows_ref.at[source, :], out_any.at[pl.ds((k - 1) * nb, nb), :], sems.at[k]
            )
            copy.start()
            copies.append(copy)
    for copy in copies:
        copy.wait()


def rounds_of(n_col):
    far = list(zip(range(n_col // 2, n_col, 2), range(n_col - 1, n_col // 2, -2)))
    return far[:0:-1] + [(by, by + 1) for by in range(2, n_col // 2, 2)] + far[:1]


def on_device(eigvecs, offsets, plan, refl_v, refl_t):
    n_row, n_col = lax.axis_size("row"), lax.axis_size("col")
    own_rows, own_cols = eigvecs.shape
    nb = refl_t.shape[2]
    n_blocks = plan.shape[1]

    def send(x, row_by, col_by):
        to = [
            (r * n_col + c, (r ^ row_by) * n_col + (c ^ col_by[r % 2]))
            for r in range(n_row)
            for c in range(n_col)
        ]
        return lax.ppermute(x, AXES, to)

    wire = pack(refl_v, refl_t)
    got = [(send(wire, 0, by), by) for by in rounds_of(n_col)]
    near = (send(wire, 0, (1, 1)), (1, 1))
    parts = {0: eigvecs}
    for step in range(2, n_row, 2):
        parts[step] = send(eigvecs, step, (0, 0))
    swaps = [(send(x, 1, (0, 0)), by[::-1]) for x, by in got]
    for step in range(0, n_row, 2):
        parts[step + 1] = send(parts[step], 1, (0, 0))
    parts = [parts[step] for step in range(n_row)]

    table = jnp.pad(plan, ((0, 7), (0, nb - n_blocks)), constant_values=offsets[0])
    vmem = pl.BlockSpec(memory_space=pltpu.VMEM)
    here = pl.BlockSpec(memory_space=pl.ANY)
    shape = jax.ShapeDtypeStruct((n_col, 8, nb, nb), BF16)
    limit = pltpu.CompilerParams(vmem_limit_bytes=max(12 * 2**20, 8 * n_blocks * 2**17))
    early, late = [(wire, (0, 0)), near] + got + swaps[:-1], swaps[-1:]
    pieces = pl.pallas_call(
        functools.partial(unpack_kernel, [by for _, by in early]),
        out_shape=shape,
        in_specs=[vmem] * len(early),
        out_specs=vmem,
        compiler_params=limit,
        name="unpack_early",
    )(*[x for x, _ in early])
    n_in = 1 + len(late) + n_row
    return pl.pallas_call(
        functools.partial(apply_kernel, [by for _, by in late], n_row, n_blocks),
        out_shape=(jax.ShapeDtypeStruct((own_rows, own_cols), F32), shape),
        in_specs=[here] + [vmem] * (len(late) + n_row + 1),
        out_specs=(here, vmem),
        scratch_shapes=[
            pltpu.VMEM((n_row * own_rows + 3 * nb, own_cols), F32),
            pltpu.VMEM((n_blocks + 4, 2, nb, own_cols), BF16),
            pltpu.SMEM((8, nb), jnp.int32),
            pltpu.SemaphoreType.DMA((1 + own_rows // nb,)),
        ],
        input_output_aliases={n_in: 1},
        compiler_params=limit,
        name="apply_blocks",
    )(table, *[x for x, _ in late], *parts, pieces)[0]


def solution(mesh):
    in_specs = (P("row", "col"), P(), P(), P("col", None, None), P("col", None, None))
    return jax.shard_map(
        on_device, mesh=mesh, in_specs=in_specs, out_specs=P("row", "col"), check_vma=False
    )
```

time: 24.2 us -> 22.3 us (0.921)
  waiting for transfers between devices: 6.7 us -> 5.46 us
  starting transfers between devices: 10.3 us -> 9.85 us
    ppermute x10, waiting for transfers between devices: 6.7 us -> 5.46 us  [send(): return lax.ppermute(x, AXES, to)]
    ppermute x10, starting transfers between devices: 10.3 us -> 9.85 us  [send(): return lax.ppermute(x, AXES, to)]
  transfers between devices with their start and end apart: 10 -> 10, of which waited for: 3 -> 2; matrix products, arithmetic and copies ran while one was open for 7% -> 8% of each run, Pallas kernels for 5% -> 7%
where the time goes in v1:
time: 22.3 us; the launch traced here: 22.1 us
  starting transfers between devices  9.85 us (44%)
  waiting for transfers between devices  5.46 us (24%)
  Pallas kernels  4.36 us (20%)
  other arithmetic  1.08 us (5%)
  between operations  0.72 us (3%)
  local copies, waits for them, and re-layouts  0.67 us (3%)
    ppermute x10, starting transfers between devices, send(): return lax.ppermute(x, AXES, to)  9.85 us
    ppermute x10, waiting for transfers between devices, send(): return lax.ppermute(x, AXES, to)  5.46 us
    pallas_call x1, Pallas kernels, on_device(): pl.pallas_call(functools.partial(apply_kernel, [by for _, by in late], n_...  2.79 us
    pallas_call x1, Pallas kernels, on_device(): pl.pallas_call(functools.partial(unpack_kernel, [by for _, by in early]),...  1.14 us
    concatenate x1, other arithmetic, pack(): jnp.concatenate([factor.reshape(nb, 1, nb), jnp.transpose(vectors, (1, 0,...  1.08 us
    pad x1, local copies, waits for them, and re-layouts, on_device(): jnp.pad(plan, ((0, 7), (0, nb - n_blocks)), constant_values=offsets[0])  0.66 us
  transfers between devices with their start and end apart: 10, of which 2 were waited for; matrix products, arithmetic and copies ran while one was open for 8% of the time, Pallas kernels for 7%

profile of v1, /device:TPU:0, one launch (start us, length us, event | category | flops | bytes accessed | tf_op | source)
XLA Modules:
  0.0 22.1 jit_solution(8308413711425059416)
XLA Ops:
  0.0 0.0 copy-start
  0.0 3.0 %collective-permute-start.3 = (f32[256,128]{1,0:T(8,128)}, f32[256,128]{1,0:T(8,128)S(1)}, u32[]{:S(2)}, u32[]{:S(2)}) collective-permute-start(f32[256,128]{1,0:T(8,128)} %refs_2_.1), channel_id=1, source_target_pairs={{0,16},{1,17},{2,18},{3,19},{4,20},{5,21},{6,22},{7,23},{8,24},{9,... | collective-permute-start | bytes 393224 | tf_op jit(solution)/shard_map/ppermute | solution.py:231
  3.0 1.1 %pad_maximum_fusion.both_any = f32[383,1,128]{2,1,0:T(1,128)S(1)} fusion(f32[255,1,128]{2,1,0:T(1,128)} %bitcast.4, f32[128,1,128]{2,1,0:T(1,128)} %bitcast.5), kind=kLoop, calls=%fused_computation | loop fusion | flops 49024 | bytes 392192 | tf_op jit(solution)/shard_map/concatenate | solution.py:39
  4.0 0.4 %pack.1.refs_0_ = f32[160,128]{1,0:T(8,128)S(1)} custom-call(f32[383,1,128]{2,1,0:T(1,128)S(1)} %pad_maximum_fusion.both_any), custom_call_target="tpu_custom_call" | custom-call | tf_op jit(solution)/shard_map/pack/pallas_call | solution.py:40
  4.5 1.6 %collective-permute-start.7 = (f32[160,128]{1,0:T(8,128)S(1)}, f32[160,128]{1,0:T(8,128)S(1)}, u32[]{:S(2)}, u32[]{:S(2)}) collective-permute-start(f32[160,128]{1,0:T(8,128)S(1)} %pack.1.refs_0_), channel_id=1, source_target_pairs={{0,2},{1,3},{2,0},{3,1},{4,6},{5,7},{6,4},{7,5},{8,11},{9,10},{10,... | collective-permute-start | bytes 245768 | tf_op jit(solution)/shard_map/ppermute | solution.py:231
  6.1 2.5 %collective-permute-start.6 = (f32[160,128]{1,0:T(8,128)S(1)}, f32[160,128]{1,0:T(8,128)S(1)}, u32[]{:S(2)}, u32[]{:S(2)}) collective-permute-start(f32[160,128]{1,0:T(8,128)S(1)} %pack.1.refs_0_), channel_id=1, source_target_pairs={{0,6},{1,7},{2,4},{3,5},{4,2},{5,3},{6,0},{7,1},{8,13},{9,12},{10,... | collective-permute-start | bytes 245768 | tf_op jit(solution)/shard_map/ppermute | solution.py:231
  8.6 1.5 %collective-permute-start.5 = (f32[160,128]{1,0:T(8,128)S(1)}, f32[160,128]{1,0:T(8,128)S(1)}, u32[]{:S(2)}, u32[]{:S(2)}) collective-permute-start(f32[160,128]{1,0:T(8,128)S(1)} %pack.1.refs_0_), channel_id=1, source_target_pairs={{0,1},{1,0},{2,3},{3,2},{4,5},{5,4},{6,7},{7,6},{8,9},{9,8},{10,11... | collective-permute-start | bytes 245768 | tf_op jit(solution)/shard_map/ppermute | solution.py:231
  10.1 0.1 collective-permute-start
  10.2 0.0 collective-permute-done.7.refs_3_
  10.2 0.0 collective-permute-start.2
  10.2 0.0 collective-permute-done.3.refs_4_
  10.3 0.5 %collective-permute-start.4 = (f32[256,128]{1,0:T(8,128)S(1)}, f32[256,128]{1,0:T(8,128)S(1)}, u32[]{:S(2)}, u32[]{:S(2)}) collective-permute-start(f32[256,128]{1,0:T(8,128)S(1)} %collective-permute-done.3.refs_4_), channel_id=1, source_target_pairs={{0,8},{1,9},{2,10},{3,11},{4,12},{5,13},{6,14},{7,15},{8,0},{9,1},... | collective-permute-start | bytes 393224 | tf_op jit(solution)/shard_map/ppermute | solution.py:231
  10.8 2.5 %collective-permute-done.6.refs_2_ = f32[160,128]{1,0:T(8,128)S(1)} collective-permute-done((f32[160,128]{1,0:T(8,128)S(1)}, f32[160,128]{1,0:T(8,128)S(1)}, u32[]{:S(2)}, u32[]{:S(2)}) %collective-permute-start.6) | collective-permute-done | bytes 81952 | tf_op jit(solution)/shard_map/ppermute | solution.py:231
  13.3 0.6 %collective-permute-start.9 = (f32[160,128]{1,0:T(8,128)S(1)}, f32[160,128]{1,0:T(8,128)S(1)}, u32[]{:S(2)}, u32[]{:S(2)}) collective-permute-start(f32[160,128]{1,0:T(8,128)S(1)} %collective-permute-done.7.refs_3_), channel_id=1, source_target_pairs={{0,8},{1,9},{2,10},{3,11},{4,12},{5,13},{6,14},{7,15},{8,0},{9,1},... | collective-permute-start | bytes 245768 | tf_op jit(solution)/shard_map/ppermute | solution.py:231
  13.9 0.0 collective-permute-done.5.refs_1_
  13.9 0.0 collective-permute-start.8
  13.9 2.9 %collective-permute-done.refs_4_ = f32[160,128]{1,0:T(8,128)S(1)} collective-permute-done((f32[160,128]{1,0:T(8,128)S(1)}, f32[160,128]{1,0:T(8,128)S(1)}, u32[]{:S(2)}, u32[]{:S(2)}) %collective-permute-start) | collective-permute-done | bytes 81952 | tf_op jit(solution)/shard_map/ppermute | solution.py:231
  16.8 0.0 collective-permute-start.1
  17.5 0.7 %pad.4.refs_0_ = s32[8,128]{1,0:T(8,128)S(1)} pad(s32[1,6]{1,0:T(1,128)} %param.7, s32[]{:T(128)} %bitcast.3), padding=0_7x0_122 | pad | bytes 4124 | tf_op jit(solution)/shard_map/jit(_pad)/pad | solution.py:244
  18.1 0.0 collective-permute-done.9.refs_6_
  18.1 0.0 collective-permute-done.8.refs_5_
  18.1 1.1 %unpack_early.1.refs_6_ = bf16[8,8,128,128]{3,2,1,0:T(8,128)(2,1)S(1)} custom-call(f32[160,128]{1,0:T(8,128)S(1)} %pack.1.refs_0_, f32[160,128]{1,0:T(8,128)S(1)} %collective-permute-done.5.refs_1_, f32[160,128]{1,0:T(8,128)S(1)} %collective-permute-done.6.refs_2_, f32[160,128]{1,0:T(8,128)S(1)} %collective-permute-done.7.refs_3_, ...), custom_call_target="tpu_custom_call" | custom-call | tf_op jit(solution)/shard_map/unpack_early/pallas_call | solution.py:250
  19.3 0.0 collective-permute-done.2.refs_3_
  19.3 0.0 collective-permute-done.1.refs_1_
  19.3 0.0 collective-permute-done.4.refs_5_
  19.3 0.0 copy-done
  19.3 2.8 %apply_blocks.1 = (f32[256,128]{1,0:T(8,128)}, bf16[8,8,128,128]{3,2,1,0:T(8,128)(2,1)S(1)}) custom-call(s32[8,128]{1,0:T(8,128)S(1)} %pad.4.refs_0_, f32[160,128]{1,0:T(8,128)S(1)} %collective-permute-done.1.refs_1_, f32[256,128]{1,0:T(8,128)S(1)} %copy-done, f32[256,128]{1,0:T(8,128)S(1)} %collective-permute-done.2.refs_3_, ...), custom_call_target="tpu_custom_call", output_to_operand_aliasing={{1}: (6, {})} | custom-call | tf_op jit(solution)/shard_map/apply_blocks/pallas_call | solution.py:259
Async XLA Ops:
  0.0 19.3 %copy-start = (f32[256,128]{1,0:T(8,128)S(1)}, f32[256,128]{1,0:T(8,128)}, u32[]{:S(2)}) copy-start(f32[256,128]{1,0:T(8,128)} %refs_2_.1) | copy-start | bytes 393220
  0.0 10.2 %collective-permute-start.3 = (f32[256,128]{1,0:T(8,128)}, f32[256,128]{1,0:T(8,128)S(1)}, u32[]{:S(2)}, u32[]{:S(2)}) collective-permute-start(f32[256,128]{1,0:T(8,128)} %refs_2_.1), channel_id=1, source_target_pairs={{0,16},{1,17},{2,18},{3,19},{4,20},{5,21},{6,22},{7,23},{8,24},{9,... | collective-permute-start | bytes 393224 | tf_op jit(solution)/shard_map/ppermute | solution.py:231
  4.5 5.8 %collective-permute-start.7 = (f32[160,128]{1,0:T(8,128)S(1)}, f32[160,128]{1,0:T(8,128)S(1)}, u32[]{:S(2)}, u32[]{:S(2)}) collective-permute-start(f32[160,128]{1,0:T(8,128)S(1)} %pack.1.refs_0_), channel_id=1, source_target_pairs={{0,2},{1,3},{2,0},{3,1},{4,6},{5,7},{6,4},{7,5},{8,11},{9,10},{10,... | collective-permute-start | bytes 245768 | tf_op jit(solution)/shard_map/ppermute | solution.py:231
  6.1 7.2 %collective-permute-start.6 = (f32[160,128]{1,0:T(8,128)S(1)}, f32[160,128]{1,0:T(8,128)S(1)}, u32[]{:S(2)}, u32[]{:S(2)}) collective-permute-start(f32[160,128]{1,0:T(8,128)S(1)} %pack.1.refs_0_), channel_id=1, source_target_pairs={{0,6},{1,7},{2,4},{3,5},{4,2},{5,3},{6,0},{7,1},{8,13},{9,12},{10,... | collective-permute-start | bytes 245768 | tf_op jit(solution)/shard_map/ppermute | solution.py:231
  8.6 5.3 %collective-permute-start.5 = (f32[160,128]{1,0:T(8,128)S(1)}, f32[160,128]{1,0:T(8,128)S(1)}, u32[]{:S(2)}, u32[]{:S(2)}) collective-permute-start(f32[160,128]{1,0:T(8,128)S(1)} %pack.1.refs_0_), channel_id=1, source_target_pairs={{0,1},{1,0},{2,3},{3,2},{4,5},{5,4},{6,7},{7,6},{8,9},{9,8},{10,11... | collective-permute-start | bytes 245768 | tf_op jit(solution)/shard_map/ppermute | solution.py:231
  10.1 6.7 %collective-permute-start = (f32[160,128]{1,0:T(8,128)S(1)}, f32[160,128]{1,0:T(8,128)S(1)}, u32[]{:S(2)}, u32[]{:S(2)}) collective-permute-start(f32[160,128]{1,0:T(8,128)S(1)} %pack.1.refs_0_), channel_id=1, source_target_pairs={{0,4},{1,5},{2,6},{3,7},{4,0},{5,1},{6,2},{7,3},{8,15},{9,14},{10,... | collective-permute-start | bytes 245768 | tf_op jit(solution)/shard_map/ppermute | solution.py:231
  10.2 9.1 %collective-permute-start.2 = (f32[256,128]{1,0:T(8,128)}, f32[256,128]{1,0:T(8,128)S(1)}, u32[]{:S(2)}, u32[]{:S(2)}) collective-permute-start(f32[256,128]{1,0:T(8,128)} %refs_2_.1), channel_id=1, source_target_pairs={{0,8},{1,9},{2,10},{3,11},{4,12},{5,13},{6,14},{7,15},{8,0},{9,1},... | collective-permute-start | bytes 393224 | tf_op jit(solution)/shard_map/ppermute | solution.py:231
  10.3 9.1 %collective-permute-start.4 = (f32[256,128]{1,0:T(8,128)S(1)}, f32[256,128]{1,0:T(8,128)S(1)}, u32[]{:S(2)}, u32[]{:S(2)}) collective-permute-start(f32[256,128]{1,0:T(8,128)S(1)} %collective-permute-done.3.refs_4_), channel_id=1, source_target_pairs={{0,8},{1,9},{2,10},{3,11},{4,12},{5,13},{6,14},{7,15},{8,0},{9,1},... | collective-permute-start | bytes 393224 | tf_op jit(solution)/shard_map/ppermute | solution.py:231
  13.3 4.8 %collective-permute-start.9 = (f32[160,128]{1,0:T(8,128)S(1)}, f32[160,128]{1,0:T(8,128)S(1)}, u32[]{:S(2)}, u32[]{:S(2)}) collective-permute-start(f32[160,128]{1,0:T(8,128)S(1)} %collective-permute-done.7.refs_3_), channel_id=1, source_target_pairs={{0,8},{1,9},{2,10},{3,11},{4,12},{5,13},{6,14},{7,15},{8,0},{9,1},... | collective-permute-start | bytes 245768 | tf_op jit(solution)/shard_map/ppermute | solution.py:231
  13.9 4.2 %collective-permute-start.8 = (f32[160,128]{1,0:T(8,128)S(1)}, f32[160,128]{1,0:T(8,128)S(1)}, u32[]{:S(2)}, u32[]{:S(2)}) collective-permute-start(f32[160,128]{1,0:T(8,128)S(1)} %collective-permute-done.6.refs_2_), channel_id=1, source_target_pairs={{0,8},{1,9},{2,10},{3,11},{4,12},{5,13},{6,14},{7,15},{8,0},{9,1},... | collective-permute-start | bytes 245768 | tf_op jit(solution)/shard_map/ppermute | solution.py:231
  16.8 2.5 %collective-permute-start.1 = (f32[160,128]{1,0:T(8,128)S(1)}, f32[160,128]{1,0:T(8,128)S(1)}, u32[]{:S(2)}, u32[]{:S(2)}) collective-permute-start(f32[160,128]{1,0:T(8,128)S(1)} %collective-permute-done.refs_4_), channel_id=1, source_target_pairs={{0,8},{1,9},{2,10},{3,11},{4,12},{5,13},{6,14},{7,15},{8,0},{9,1},... | collective-permute-start | bytes 245768 | tf_op jit(solution)/shard_map/ppermute | solution.py:231

commit v2 on v1

--- a/solution.py
+++ b/solution.py
@@ -58,7 +58,9 @@
 
 
 def dot3(a, b):
-    return dot(a[0], b[0]) + (dot(a[1], b[0]) + dot(a[0], b[1]))
+    n = b[0].shape[1]
+    both = dot(a[0], jnp.concatenate(b, axis=1))
+    return both[:, :n] + (both[:, n:] + dot(a[1], b[0]))
 
 
 def twice(pair):
@@ -192,14 +194,18 @@
 
     mine = my_row * own_rows
     tile = lax.div(mine - first + nb, nb) - 1
-    copies = []
+    windows, values = [], []
     for k in range(own_rows // nb + 1):
         t = jnp.minimum(tile + k, n_blocks + 1)
-        low_entry = plan_ref[0, jnp.clip(t, 0, n_blocks - 1)]
-        up_entry = plan_ref[0, jnp.clip(t - 1, 0, n_blocks - 1)]
-        window = pl.ds(first + (t + 1) * nb, nb)
-        moved = dot3(up_of(up_entry), solved_of(t - 1)) + dot3(low_of(low_entry), solved_of(t))
-        rows_ref[window, :] = rows_ref[window, :] - moved
+        low = low_of(plan_ref[0, jnp.clip(t, 0, n_blocks - 1)])
+        up = up_of(plan_ref[0, jnp.clip(t - 1, 0, n_blocks - 1)])
+        both = [jnp.concatenate([up[i], low[i]], axis=1) for i in range(2)]
+        solved = [jnp.concatenate([solved_of(t - 1)[i], solved_of(t)[i]], axis=0) for i in range(2)]
+        windows.append(pl.ds(first + (t + 1) * nb, nb))
+        values.append(rows_ref[windows[-1], :] - dot3(both, solved))
+    copies = []
+    for k, (window, value) in enumerate(zip(windows, values)):
+        rows_ref[window, :] = value
         if k > 0:
             source = pl.ds(pl.multiple_of(mine + k * nb, nb), nb)
             copy = pltpu.make_async_copy(

time: 22.3 us -> 22.1 us (level)
    pallas_call x1, Pallas kernels: 2.79 us -> 2.55 us  [on_device(): pl.pallas_call(functools.partial(apply_kernel, [by for _, by in late], n_...]
where the time goes in v2:
time: 22.1 us; the launch traced here: 21.9 us
  starting transfers between devices  9.85 us (45%)
  waiting for transfers between devices  5.46 us (25%)
  Pallas kernels  4.16 us (19%)
  other arithmetic  1.08 us (5%)
  between operations  0.72 us (3%)
  local copies, waits for them, and re-layouts  0.67 us (3%)
    ppermute x10, starting transfers between devices, send(): return lax.ppermute(x, AXES, to)  9.85 us
    ppermute x10, waiting for transfers between devices, send(): return lax.ppermute(x, AXES, to)  5.46 us
    pallas_call x1, Pallas kernels, on_device(): pl.pallas_call(functools.partial(apply_kernel, [by for _, by in late], n_...  2.55 us
    pallas_call x1, Pallas kernels, on_device(): pl.pallas_call(functools.partial(unpack_kernel, [by for _, by in early]),...  1.18 us
    concatenate x1, other arithmetic, pack(): jnp.concatenate([factor.reshape(nb, 1, nb), jnp.transpose(vectors, (1, 0,...  1.08 us
    pad x1, local copies, waits for them, and re-layouts, on_device(): jnp.pad(plan, ((0, 7), (0, nb - n_blocks)), constant_values=offsets[0])  0.66 us
  transfers between devices with their start and end apart: 10, of which 2 were waited for; matrix products, arithmetic and copies ran while one was open for 8% of the time, Pallas kernels for 7%

profile of v2, /device:TPU:0, one launch (start us, length us, event | category | flops | bytes accessed | tf_op | source)
XLA Modules:
  0.0 21.9 jit_solution(8437461483522852038)
XLA Ops:
  0.0 0.0 copy-start
  0.0 3.0 %collective-permute-start.3 = (f32[256,128]{1,0:T(8,128)}, f32[256,128]{1,0:T(8,128)S(1)}, u32[]{:S(2)}, u32[]{:S(2)}) collective-permute-start(f32[256,128]{1,0:T(8,128)} %refs_2_.1), channel_id=1, source_target_pairs={{0,16},{1,17},{2,18},{3,19},{4,20},{5,21},{6,22},{7,23},{8,24},{9,... | collective-permute-start | bytes 393224 | tf_op jit(solution)/shard_map/ppermute | solution.py:237
  3.0 1.1 %pad_maximum_fusion.both_any = f32[383,1,128]{2,1,0:T(1,128)S(1)} fusion(f32[255,1,128]{2,1,0:T(1,128)} %bitcast.4, f32[128,1,128]{2,1,0:T(1,128)} %bitcast.5), kind=kLoop, calls=%fused_computation | loop fusion | flops 49024 | bytes 392192 | tf_op jit(solution)/shard_map/concatenate | solution.py:39
  4.0 0.4 %pack.1.refs_0_ = f32[160,128]{1,0:T(8,128)S(1)} custom-call(f32[383,1,128]{2,1,0:T(1,128)S(1)} %pad_maximum_fusion.both_any), custom_call_target="tpu_custom_call" | custom-call | tf_op jit(solution)/shard_map/pack/pallas_call | solution.py:40
  4.5 1.6 %collective-permute-start.7 = (f32[160,128]{1,0:T(8,128)S(1)}, f32[160,128]{1,0:T(8,128)S(1)}, u32[]{:S(2)}, u32[]{:S(2)}) collective-permute-start(f32[160,128]{1,0:T(8,128)S(1)} %pack.1.refs_0_), channel_id=1, source_target_pairs={{0,2},{1,3},{2,0},{3,1},{4,6},{5,7},{6,4},{7,5},{8,11},{9,10},{10,... | collective-permute-start | bytes 245768 | tf_op jit(solution)/shard_map/ppermute | solution.py:237
  6.1 2.5 %collective-permute-start.6 = (f32[160,128]{1,0:T(8,128)S(1)}, f32[160,128]{1,0:T(8,128)S(1)}, u32[]{:S(2)}, u32[]{:S(2)}) collective-permute-start(f32[160,128]{1,0:T(8,128)S(1)} %pack.1.refs_0_), channel_id=1, source_target_pairs={{0,6},{1,7},{2,4},{3,5},{4,2},{5,3},{6,0},{7,1},{8,13},{9,12},{10,... | collective-permute-start | bytes 245768 | tf_op jit(solution)/shard_map/ppermute | solution.py:237
  8.6 1.5 %collective-permute-start.5 = (f32[160,128]{1,0:T(8,128)S(1)}, f32[160,128]{1,0:T(8,128)S(1)}, u32[]{:S(2)}, u32[]{:S(2)}) collective-permute-start(f32[160,128]{1,0:T(8,128)S(1)} %pack.1.refs_0_), channel_id=1, source_target_pairs={{0,1},{1,0},{2,3},{3,2},{4,5},{5,4},{6,7},{7,6},{8,9},{9,8},{10,11... | collective-permute-start | bytes 245768 | tf_op jit(solution)/shard_map/ppermute | solution.py:237
  10.1 0.1 collective-permute-start
  10.2 0.0 collective-permute-done.7.refs_3_
  10.2 0.0 collective-permute-start.2
  10.2 0.0 collective-permute-done.3.refs_4_
  10.3 0.5 %collective-permute-start.4 = (f32[256,128]{1,0:T(8,128)S(1)}, f32[256,128]{1,0:T(8,128)S(1)}, u32[]{:S(2)}, u32[]{:S(2)}) collective-permute-start(f32[256,128]{1,0:T(8,128)S(1)} %collective-permute-done.3.refs_4_), channel_id=1, source_target_pairs={{0,8},{1,9},{2,10},{3,11},{4,12},{5,13},{6,14},{7,15},{8,0},{9,1},... | collective-permute-start | bytes 393224 | tf_op jit(solution)/shard_map/ppermute | solution.py:237
  10.8 2.5 %collective-permute-done.6.refs_2_ = f32[160,128]{1,0:T(8,128)S(1)} collective-permute-done((f32[160,128]{1,0:T(8,128)S(1)}, f32[160,128]{1,0:T(8,128)S(1)}, u32[]{:S(2)}, u32[]{:S(2)}) %collective-permute-start.6) | collective-permute-done | bytes 81952 | tf_op jit(solution)/shard_map/ppermute | solution.py:237
  13.3 0.6 %collective-permute-start.9 = (f32[160,128]{1,0:T(8,128)S(1)}, f32[160,128]{1,0:T(8,128)S(1)}, u32[]{:S(2)}, u32[]{:S(2)}) collective-permute-start(f32[160,128]{1,0:T(8,128)S(1)} %collective-permute-done.7.refs_3_), channel_id=1, source_target_pairs={{0,8},{1,9},{2,10},{3,11},{4,12},{5,13},{6,14},{7,15},{8,0},{9,1},... | collective-permute-start | bytes 245768 | tf_op jit(solution)/shard_map/ppermute | solution.py:237
  13.9 0.0 collective-permute-done.5.refs_1_
  13.9 0.0 collective-permute-start.8
  13.9 2.9 %collective-permute-done.refs_4_ = f32[160,128]{1,0:T(8,128)S(1)} collective-permute-done((f32[160,128]{1,0:T(8,128)S(1)}, f32[160,128]{1,0:T(8,128)S(1)}, u32[]{:S(2)}, u32[]{:S(2)}) %collective-permute-start) | collective-permute-done | bytes 81952 | tf_op jit(solution)/shard_map/ppermute | solution.py:237
  16.8 0.0 collective-permute-start.1
  17.5 0.7 %pad.4.refs_0_ = s32[8,128]{1,0:T(8,128)S(1)} pad(s32[1,6]{1,0:T(1,128)} %param.7, s32[]{:T(128)} %bitcast.3), padding=0_7x0_122 | pad | bytes 4124 | tf_op jit(solution)/shard_map/jit(_pad)/pad | solution.py:250
  18.1 0.0 collective-permute-done.9.refs_6_
  18.1 0.0 collective-permute-done.8.refs_5_
  18.1 1.2 %unpack_early.1.refs_6_ = bf16[8,8,128,128]{3,2,1,0:T(8,128)(2,1)S(1)} custom-call(f32[160,128]{1,0:T(8,128)S(1)} %pack.1.refs_0_, f32[160,128]{1,0:T(8,128)S(1)} %collective-permute-done.5.refs_1_, f32[160,128]{1,0:T(8,128)S(1)} %collective-permute-done.6.refs_2_, f32[160,128]{1,0:T(8,128)S(1)} %collective-permute-done.7.refs_3_, ...), custom_call_target="tpu_custom_call" | custom-call | tf_op jit(solution)/shard_map/unpack_early/pallas_call | solution.py:256
  19.3 0.0 collective-permute-done.2.refs_3_
  19.3 0.0 collective-permute-done.1.refs_1_
  19.4 0.0 collective-permute-done.4.refs_5_
  19.4 0.0 copy-done
  19.4 2.5 %apply_blocks.1 = (f32[256,128]{1,0:T(8,128)}, bf16[8,8,128,128]{3,2,1,0:T(8,128)(2,1)S(1)}) custom-call(s32[8,128]{1,0:T(8,128)S(1)} %pad.4.refs_0_, f32[160,128]{1,0:T(8,128)S(1)} %collective-permute-done.1.refs_1_, f32[256,128]{1,0:T(8,128)S(1)} %copy-done, f32[256,128]{1,0:T(8,128)S(1)} %collective-permute-done.2.refs_3_, ...), custom_call_target="tpu_custom_call", output_to_operand_aliasing={{1}: (6, {})} | custom-call | tf_op jit(solution)/shard_map/apply_blocks/pallas_call | solution.py:265
Async XLA Ops:
  0.0 19.4 %copy-start = (f32[256,128]{1,0:T(8,128)S(1)}, f32[256,128]{1,0:T(8,128)}, u32[]{:S(2)}) copy-start(f32[256,128]{1,0:T(8,128)} %refs_2_.1) | copy-start | bytes 393220
  0.0 10.2 %collective-permute-start.3 = (f32[256,128]{1,0:T(8,128)}, f32[256,128]{1,0:T(8,128)S(1)}, u32[]{:S(2)}, u32[]{:S(2)}) collective-permute-start(f32[256,128]{1,0:T(8,128)} %refs_2_.1), channel_id=1, source_target_pairs={{0,16},{1,17},{2,18},{3,19},{4,20},{5,21},{6,22},{7,23},{8,24},{9,... | collective-permute-start | bytes 393224 | tf_op jit(solution)/shard_map/ppermute | solution.py:237
  4.5 5.8 %collective-permute-start.7 = (f32[160,128]{1,0:T(8,128)S(1)}, f32[160,128]{1,0:T(8,128)S(1)}, u32[]{:S(2)}, u32[]{:S(2)}) collective-permute-start(f32[160,128]{1,0:T(8,128)S(1)} %pack.1.refs_0_), channel_id=1, source_target_pairs={{0,2},{1,3},{2,0},{3,1},{4,6},{5,7},{6,4},{7,5},{8,11},{9,10},{10,... | collective-permute-start | bytes 245768 | tf_op jit(solution)/shard_map/ppermute | solution.py:237
  6.1 7.2 %collective-permute-start.6 = (f32[160,128]{1,0:T(8,128)S(1)}, f32[160,128]{1,0:T(8,128)S(1)}, u32[]{:S(2)}, u32[]{:S(2)}) collective-permute-start(f32[160,128]{1,0:T(8,128)S(1)} %pack.1.refs_0_), channel_id=1, source_target_pairs={{0,6},{1,7},{2,4},{3,5},{4,2},{5,3},{6,0},{7,1},{8,13},{9,12},{10,... | collective-permute-start | bytes 245768 | tf_op jit(solution)/shard_map/ppermute | solution.py:237
  8.6 5.3 %collective-permute-start.5 = (f32[160,128]{1,0:T(8,128)S(1)}, f32[160,128]{1,0:T(8,128)S(1)}, u32[]{:S(2)}, u32[]{:S(2)}) collective-permute-start(f32[160,128]{1,0:T(8,128)S(1)} %pack.1.refs_0_), channel_id=1, source_target_pairs={{0,1},{1,0},{2,3},{3,2},{4,5},{5,4},{6,7},{7,6},{8,9},{9,8},{10,11... | collective-permute-start | bytes 245768 | tf_op jit(solution)/shard_map/ppermute | solution.py:237
  10.1 6.7 %collective-permute-start = (f32[160,128]{1,0:T(8,128)S(1)}, f32[160,128]{1,0:T(8,128)S(1)}, u32[]{:S(2)}, u32[]{:S(2)}) collective-permute-start(f32[160,128]{1,0:T(8,128)S(1)} %pack.1.refs_0_), channel_id=1, source_target_pairs={{0,4},{1,5},{2,6},{3,7},{4,0},{5,1},{6,2},{7,3},{8,15},{9,14},{10,... | collective-permute-start | bytes 245768 | tf_op jit(solution)/shard_map/ppermute | solution.py:237
  10.2 9.1 %collective-permute-start.2 = (f32[256,128]{1,0:T(8,128)}, f32[256,128]{1,0:T(8,128)S(1)}, u32[]{:S(2)}, u32[]{:S(2)}) collective-permute-start(f32[256,128]{1,0:T(8,128)} %refs_2_.1), channel_id=1, source_target_pairs={{0,8},{1,9},{2,10},{3,11},{4,12},{5,13},{6,14},{7,15},{8,0},{9,1},... | collective-permute-start | bytes 393224 | tf_op jit(solution)/shard_map/ppermute | solution.py:237
  10.3 9.1 %collective-permute-start.4 = (f32[256,128]{1,0:T(8,128)S(1)}, f32[256,128]{1,0:T(8,128)S(1)}, u32[]{:S(2)}, u32[]{:S(2)}) collective-permute-start(f32[256,128]{1,0:T(8,128)S(1)} %collective-permute-done.3.refs_4_), channel_id=1, source_target_pairs={{0,8},{1,9},{2,10},{3,11},{4,12},{5,13},{6,14},{7,15},{8,0},{9,1},... | collective-permute-start | bytes 393224 | tf_op jit(solution)/shard_map/ppermute | solution.py:237
  13.3 4.8 %collective-permute-start.9 = (f32[160,128]{1,0:T(8,128)S(1)}, f32[160,128]{1,0:T(8,128)S(1)}, u32[]{:S(2)}, u32[]{:S(2)}) collective-permute-start(f32[160,128]{1,0:T(8,128)S(1)} %collective-permute-done.7.refs_3_), channel_id=1, source_target_pairs={{0,8},{1,9},{2,10},{3,11},{4,12},{5,13},{6,14},{7,15},{8,0},{9,1},... | collective-permute-start | bytes 245768 | tf_op jit(solution)/shard_map/ppermute | solution.py:237
  13.9 4.2 %collective-permute-start.8 = (f32[160,128]{1,0:T(8,128)S(1)}, f32[160,128]{1,0:T(8,128)S(1)}, u32[]{:S(2)}, u32[]{:S(2)}) collective-permute-start(f32[160,128]{1,0:T(8,128)S(1)} %collective-permute-done.6.refs_2_), channel_id=1, source_target_pairs={{0,8},{1,9},{2,10},{3,11},{4,12},{5,13},{6,14},{7,15},{8,0},{9,1},... | collective-permute-start | bytes 245768 | tf_op jit(solution)/shard_map/ppermute | solution.py:237
  16.8 2.5 %collective-permute-start.1 = (f32[160,128]{1,0:T(8,128)S(1)}, f32[160,128]{1,0:T(8,128)S(1)}, u32[]{:S(2)}, u32[]{:S(2)}) collective-permute-start(f32[160,128]{1,0:T(8,128)S(1)} %collective-permute-done.refs_4_), channel_id=1, source_target_pairs={{0,8},{1,9},{2,10},{3,11},{4,12},{5,13},{6,14},{7,15},{8,0},{9,1},... | collective-permute-start | bytes 245768 | tf_op jit(solution)/shard_map/ppermute | solution.py:237

commit v3 on v2

--- a/solution.py
+++ b/solution.py
@@ -16,16 +16,13 @@
     return lax.broadcasted_iota(jnp.int32, (rows, cols), 0), lax.broadcasted_iota(jnp.int32, (rows, cols), 1)
 
 
-def pack_kernel(both_any, wire_ref, both_ref, sem):
+def pack_kernel(both_ref, wire_ref):
     nb = wire_ref.shape[1]
     half, quarter = nb // 2, nb // 4
-    copy = pltpu.make_async_copy(both_any.at[:, 0, :], both_ref.at[0 : 3 * nb - 1], sem)
-    copy.start()
-    copy.wait()
     row, col = iotas(nb, nb)
-    factor = both_ref[0:nb, :]
-    low = both_ref[nb : 2 * nb, :]
-    up = pltpu.roll(both_ref[2 * nb - 1 : 3 * nb - 1, :], nb - 1, axis=0)
+    factor = both_ref[0:nb, 0, :]
+    low = both_ref[nb : 2 * nb, 0, :]
+    up = pltpu.roll(both_ref[2 * nb - 1 : 3 * nb - 1, 0, :], nb - 1, axis=0)
     wire_ref[0:nb, :] = jnp.where(row > col, low, jnp.where(row < col, up, factor))
     turned = jnp.transpose(jnp.concatenate([factor[half:, :], factor[:half, :]], axis=0))[half:, :]
     row, col = iotas(half, nb)
@@ -40,9 +37,6 @@
     return pl.pallas_call(
         pack_kernel,
         out_shape=jax.ShapeDtypeStruct((nb + nb // 4, nb), F32),
-        in_specs=[pl.BlockSpec(memory_space=pl.ANY)],
-        out_specs=pl.BlockSpec(memory_space=pltpu.VMEM),
-        scratch_shapes=[pltpu.VMEM((3 * nb, nb), F32), pltpu.SemaphoreType.DMA],
         compiler_params=pltpu.CompilerParams(vmem_limit_bytes=4 * 2**20),
         name="pack",
     )(both)
@@ -219,7 +213,7 @@
 
 def rounds_of(n_col):
     far = list(zip(range(n_col // 2, n_col, 2), range(n_col - 1, n_col // 2, -2)))
-    return far[:0:-1] + [(by, by + 1) for by in range(2, n_col // 2, 2)] + far[:1]
+    return far[:0:-1] + [(by + 1, by) for by in range(2, n_col // 2, 2)] + far[:1]
 
 
 def on_device(eigvecs, offsets, plan, refl_v, refl_t):

time: 22.1 us -> 21.9 us (level)
  waiting for transfers between devices: 5.46 us -> 6.18 us
  starting transfers between devices: 9.85 us -> 9.13 us
  Pallas kernels: 4.16 us -> 3.93 us
    ppermute x10, waiting for transfers between devices: 5.46 us -> 6.18 us  [send(): return lax.ppermute(x, AXES, to)]
    ppermute x10, starting transfers between devices: 9.85 us -> 9.13 us  [send(): return lax.ppermute(x, AXES, to)]
    pallas_call x1, Pallas kernels: 0.43 us -> 0.19 us  [pack(): pl.pallas_call(pack_kernel, out_shape=jax.ShapeDtypeStruct((nb + nb // 4,...]
  transfers between devices with their start and end apart: 10 -> 10, of which waited for: 2 -> 3; matrix products, arithmetic and copies ran while one was open for 8% -> 8% of each run, Pallas kernels for 7% -> 6%
where the time goes in v3:
time: 21.9 us; the launch traced here: 21.7 us
  starting transfers between devices  9.13 us (42%)
  waiting for transfers between devices  6.18 us (28%)
  Pallas kernels  3.93 us (18%)
  other arithmetic  1.08 us (5%)
  between operations  0.71 us (3%)
  local copies, waits for them, and re-layouts  0.67 us (3%)
    ppermute x10, starting transfers between devices, send(): return lax.ppermute(x, AXES, to)  9.13 us
    ppermute x10, waiting for transfers between devices, send(): return lax.ppermute(x, AXES, to)  6.18 us
    pallas_call x1, Pallas kernels, on_device(): pl.pallas_call(functools.partial(apply_kernel, [by for _, by in late], n_...  2.55 us
    pallas_call x1, Pallas kernels, on_device(): pl.pallas_call(functools.partial(unpack_kernel, [by for _, by in early]),...  1.18 us
    concatenate x1, other arithmetic, pack(): jnp.concatenate([factor.reshape(nb, 1, nb), jnp.transpose(vectors, (1, 0,...  1.08 us
    pad x1, local copies, waits for them, and re-layouts, on_device(): jnp.pad(plan, ((0, 7), (0, nb - n_blocks)), constant_values=offsets[0])  0.66 us
  transfers between devices with their start and end apart: 10, of which 3 were waited for; matrix products, arithmetic and copies ran while one was open for 8% of the time, Pallas kernels for 6%

profile of v3, /device:TPU:0, one launch (start us, length us, event | category | flops | bytes accessed | tf_op | source)
XLA Modules:
  0.0 21.7 jit_solution(1902969590210480422)
XLA Ops:
  0.0 0.0 copy-start
  0.0 3.0 %collective-permute-start.3 = (f32[256,128]{1,0:T(8,128)}, f32[256,128]{1,0:T(8,128)S(1)}, u32[]{:S(2)}, u32[]{:S(2)}) collective-permute-start(f32[256,128]{1,0:T(8,128)} %refs_2_.1), channel_id=1, source_target_pairs={{0,16},{1,17},{2,18},{3,19},{4,20},{5,21},{6,22},{7,23},{8,24},{9,... | collective-permute-start | bytes 393224 | tf_op jit(solution)/shard_map/ppermute | solution.py:231
  3.0 1.1 %pad_maximum_fusion.both_ref = f32[383,1,128]{2,1,0:T(1,128)S(1)} fusion(f32[255,1,128]{2,1,0:T(1,128)} %bitcast.4, f32[128,1,128]{2,1,0:T(1,128)} %bitcast.5), kind=kLoop, calls=%fused_computation | loop fusion | flops 49024 | bytes 392192 | tf_op jit(solution)/shard_map/concatenate | solution.py:36
  4.0 0.2 pack.1.refs_0_
  4.2 2.6 %collective-permute-start.7 = (f32[160,128]{1,0:T(8,128)S(1)}, f32[160,128]{1,0:T(8,128)S(1)}, u32[]{:S(2)}, u32[]{:S(2)}) collective-permute-start(f32[160,128]{1,0:T(8,128)S(1)} %pack.1.refs_0_), channel_id=1, source_target_pairs={{0,3},{1,2},{2,1},{3,0},{4,7},{5,6},{6,5},{7,4},{8,10},{9,11},{10,... | collective-permute-start | bytes 245768 | tf_op jit(solution)/shard_map/ppermute | solution.py:231
  6.8 2.5 %collective-permute-start.6 = (f32[160,128]{1,0:T(8,128)S(1)}, f32[160,128]{1,0:T(8,128)S(1)}, u32[]{:S(2)}, u32[]{:S(2)}) collective-permute-start(f32[160,128]{1,0:T(8,128)S(1)} %pack.1.refs_0_), channel_id=1, source_target_pairs={{0,6},{1,7},{2,4},{3,5},{4,2},{5,3},{6,0},{7,1},{8,13},{9,12},{10,... | collective-permute-start | bytes 245768 | tf_op jit(solution)/shard_map/ppermute | solution.py:231
  9.3 0.5 %collective-permute-start.5 = (f32[160,128]{1,0:T(8,128)S(1)}, f32[160,128]{1,0:T(8,128)S(1)}, u32[]{:S(2)}, u32[]{:S(2)}) collective-permute-start(f32[160,128]{1,0:T(8,128)S(1)} %pack.1.refs_0_), channel_id=1, source_target_pairs={{0,1},{1,0},{2,3},{3,2},{4,5},{5,4},{6,7},{7,6},{8,9},{9,8},{10,11... | collective-permute-start | bytes 245768 | tf_op jit(solution)/shard_map/ppermute | solution.py:231
  9.8 0.1 collective-permute-start
  9.9 0.0 collective-permute-done.7.refs_3_
  9.9 0.0 collective-permute-start.2
  9.9 0.0 collective-permute-done.3.refs_4_
  9.9 0.5 %collective-permute-start.4 = (f32[256,128]{1,0:T(8,128)S(1)}, f32[256,128]{1,0:T(8,128)S(1)}, u32[]{:S(2)}, u32[]{:S(2)}) collective-permute-start(f32[256,128]{1,0:T(8,128)S(1)} %collective-permute-done.3.refs_4_), channel_id=1, source_target_pairs={{0,8},{1,9},{2,10},{3,11},{4,12},{5,13},{6,14},{7,15},{8,0},{9,1},... | collective-permute-start | bytes 393224 | tf_op jit(solution)/shard_map/ppermute | solution.py:231
  10.4 2.7 %collective-permute-done.6.refs_2_ = f32[160,128]{1,0:T(8,128)S(1)} collective-permute-done((f32[160,128]{1,0:T(8,128)S(1)}, f32[160,128]{1,0:T(8,128)S(1)}, u32[]{:S(2)}, u32[]{:S(2)}) %collective-permute-start.6) | collective-permute-done | bytes 81952 | tf_op jit(solution)/shard_map/ppermute | solution.py:231
  13.1 0.0 collective-permute-start.9
  13.1 0.6 %collective-permute-done.5.refs_1_ = f32[160,128]{1,0:T(8,128)S(1)} collective-permute-done((f32[160,128]{1,0:T(8,128)S(1)}, f32[160,128]{1,0:T(8,128)S(1)}, u32[]{:S(2)}, u32[]{:S(2)}) %collective-permute-start.5) | collective-permute-done | bytes 81952 | tf_op jit(solution)/shard_map/ppermute | solution.py:231
  13.7 0.0 collective-permute-start.8
  13.7 2.9 %collective-permute-done.refs_4_ = f32[160,128]{1,0:T(8,128)S(1)} collective-permute-done((f32[160,128]{1,0:T(8,128)S(1)}, f32[160,128]{1,0:T(8,128)S(1)}, u32[]{:S(2)}, u32[]{:S(2)}) %collective-permute-start) | collective-permute-done | bytes 81952 | tf_op jit(solution)/shard_map/ppermute | solution.py:231
  16.6 0.0 collective-permute-start.1
  17.2 0.7 %pad.4.refs_0_ = s32[8,128]{1,0:T(8,128)S(1)} pad(s32[1,6]{1,0:T(1,128)} %param.7, s32[]{:T(128)} %bitcast.3), padding=0_7x0_122 | pad | bytes 4124 | tf_op jit(solution)/shard_map/jit(_pad)/pad | solution.py:244
  17.9 0.0 collective-permute-done.9.refs_6_
  17.9 0.0 collective-permute-done.8.refs_5_
  17.9 1.2 %unpack_early.1.refs_6_ = bf16[8,8,128,128]{3,2,1,0:T(8,128)(2,1)S(1)} custom-call(f32[160,128]{1,0:T(8,128)S(1)} %pack.1.refs_0_, f32[160,128]{1,0:T(8,128)S(1)} %collective-permute-done.5.refs_1_, f32[160,128]{1,0:T(8,128)S(1)} %collective-permute-done.6.refs_2_, f32[160,128]{1,0:T(8,128)S(1)} %collective-permute-done.7.refs_3_, ...), custom_call_target="tpu_custom_call" | custom-call | tf_op jit(solution)/shard_map/unpack_early/pallas_call | solution.py:250
  19.1 0.0 collective-permute-done.2.refs_3_
  19.1 0.0 collective-permute-done.1.refs_1_
  19.1 0.0 collective-permute-done.4.refs_5_
  19.1 0.0 copy-done
  19.1 2.6 %apply_blocks.1 = (f32[256,128]{1,0:T(8,128)}, bf16[8,8,128,128]{3,2,1,0:T(8,128)(2,1)S(1)}) custom-call(s32[8,128]{1,0:T(8,128)S(1)} %pad.4.refs_0_, f32[160,128]{1,0:T(8,128)S(1)} %collective-permute-done.1.refs_1_, f32[256,128]{1,0:T(8,128)S(1)} %copy-done, f32[256,128]{1,0:T(8,128)S(1)} %collective-permute-done.2.refs_3_, ...), custom_call_target="tpu_custom_call", output_to_operand_aliasing={{1}: (6, {})} | custom-call | tf_op jit(solution)/shard_map/apply_blocks/pallas_call | solution.py:259
Async XLA Ops:
  0.0 19.1 %copy-start = (f32[256,128]{1,0:T(8,128)S(1)}, f32[256,128]{1,0:T(8,128)}, u32[]{:S(2)}) copy-start(f32[256,128]{1,0:T(8,128)} %refs_2_.1) | copy-start | bytes 393220
  0.0 9.9 %collective-permute-start.3 = (f32[256,128]{1,0:T(8,128)}, f32[256,128]{1,0:T(8,128)S(1)}, u32[]{:S(2)}, u32[]{:S(2)}) collective-permute-start(f32[256,128]{1,0:T(8,128)} %refs_2_.1), channel_id=1, source_target_pairs={{0,16},{1,17},{2,18},{3,19},{4,20},{5,21},{6,22},{7,23},{8,24},{9,... | collective-permute-start | bytes 393224 | tf_op jit(solution)/shard_map/ppermute | solution.py:231
  4.2 5.7 %collective-permute-start.7 = (f32[160,128]{1,0:T(8,128)S(1)}, f32[160,128]{1,0:T(8,128)S(1)}, u32[]{:S(2)}, u32[]{:S(2)}) collective-permute-start(f32[160,128]{1,0:T(8,128)S(1)} %pack.1.refs_0_), channel_id=1, source_target_pairs={{0,3},{1,2},{2,1},{3,0},{4,7},{5,6},{6,5},{7,4},{8,10},{9,11},{10,... | collective-permute-start | bytes 245768 | tf_op jit(solution)/shard_map/ppermute | solution.py:231
  6.8 6.3 %collective-permute-start.6 = (f32[160,128]{1,0:T(8,128)S(1)}, f32[160,128]{1,0:T(8,128)S(1)}, u32[]{:S(2)}, u32[]{:S(2)}) collective-permute-start(f32[160,128]{1,0:T(8,128)S(1)} %pack.1.refs_0_), channel_id=1, source_target_pairs={{0,6},{1,7},{2,4},{3,5},{4,2},{5,3},{6,0},{7,1},{8,13},{9,12},{10,... | collective-permute-start | bytes 245768 | tf_op jit(solution)/shard_map/ppermute | solution.py:231
  9.3 4.4 %collective-permute-start.5 = (f32[160,128]{1,0:T(8,128)S(1)}, f32[160,128]{1,0:T(8,128)S(1)}, u32[]{:S(2)}, u32[]{:S(2)}) collective-permute-start(f32[160,128]{1,0:T(8,128)S(1)} %pack.1.refs_0_), channel_id=1, source_target_pairs={{0,1},{1,0},{2,3},{3,2},{4,5},{5,4},{6,7},{7,6},{8,9},{9,8},{10,11... | collective-permute-start | bytes 245768 | tf_op jit(solution)/shard_map/ppermute | solution.py:231
  9.8 6.8 %collective-permute-start = (f32[160,128]{1,0:T(8,128)S(1)}, f32[160,128]{1,0:T(8,128)S(1)}, u32[]{:S(2)}, u32[]{:S(2)}) collective-permute-start(f32[160,128]{1,0:T(8,128)S(1)} %pack.1.refs_0_), channel_id=1, source_target_pairs={{0,4},{1,5},{2,6},{3,7},{4,0},{5,1},{6,2},{7,3},{8,15},{9,14},{10,... | collective-permute-start | bytes 245768 | tf_op jit(solution)/shard_map/ppermute | solution.py:231
  9.9 9.2 %collective-permute-start.2 = (f32[256,128]{1,0:T(8,128)}, f32[256,128]{1,0:T(8,128)S(1)}, u32[]{:S(2)}, u32[]{:S(2)}) collective-permute-start(f32[256,128]{1,0:T(8,128)} %refs_2_.1), channel_id=1, source_target_pairs={{0,8},{1,9},{2,10},{3,11},{4,12},{5,13},{6,14},{7,15},{8,0},{9,1},... | collective-permute-start | bytes 393224 | tf_op jit(solution)/shard_map/ppermute | solution.py:231
  9.9 9.2 %collective-permute-start.4 = (f32[256,128]{1,0:T(8,128)S(1)}, f32[256,128]{1,0:T(8,128)S(1)}, u32[]{:S(2)}, u32[]{:S(2)}) collective-permute-start(f32[256,128]{1,0:T(8,128)S(1)} %collective-permute-done.3.refs_4_), channel_id=1, source_target_pairs={{0,8},{1,9},{2,10},{3,11},{4,12},{5,13},{6,14},{7,15},{8,0},{9,1},... | collective-permute-start | bytes 393224 | tf_op jit(solution)/shard_map/ppermute | solution.py:231
  13.1 4.8 %collective-permute-start.9 = (f32[160,128]{1,0:T(8,128)S(1)}, f32[160,128]{1,0:T(8,128)S(1)}, u32[]{:S(2)}, u32[]{:S(2)}) collective-permute-start(f32[160,128]{1,0:T(8,128)S(1)} %collective-permute-done.7.refs_3_), channel_id=1, source_target_pairs={{0,8},{1,9},{2,10},{3,11},{4,12},{5,13},{6,14},{7,15},{8,0},{9,1},... | collective-permute-start | bytes 245768 | tf_op jit(solution)/shard_map/ppermute | solution.py:231
  13.7 4.2 %collective-permute-start.8 = (f32[160,128]{1,0:T(8,128)S(1)}, f32[160,128]{1,0:T(8,128)S(1)}, u32[]{:S(2)}, u32[]{:S(2)}) collective-permute-start(f32[160,128]{1,0:T(8,128)S(1)} %collective-permute-done.6.refs_2_), channel_id=1, source_target_pairs={{0,8},{1,9},{2,10},{3,11},{4,12},{5,13},{6,14},{7,15},{8,0},{9,1},... | collective-permute-start | bytes 245768 | tf_op jit(solution)/shard_map/ppermute | solution.py:231
  16.6 2.5 %collective-permute-start.1 = (f32[160,128]{1,0:T(8,128)S(1)}, f32[160,128]{1,0:T(8,128)S(1)}, u32[]{:S(2)}, u32[]{:S(2)}) collective-permute-start(f32[160,128]{1,0:T(8,128)S(1)} %collective-permute-done.refs_4_), channel_id=1, source_target_pairs={{0,8},{1,9},{2,10},{3,11},{4,12},{5,13},{6,14},{7,15},{8,0},{9,1},... | collective-permute-start | bytes 245768 | tf_op jit(solution)/shard_map/ppermute | solution.py:231

commit v4 on v3

--- a/solution.py
+++ b/solution.py
@@ -112,6 +112,14 @@
     unpack_into(refs[-1], refs[: len(distances)], distances)
 
 
+def dot_deep(a, b):
+    return jnp.dot(
+        jnp.concatenate([a[0], a[1], a[0]], axis=1),
+        jnp.concatenate([b[0], b[0], b[1]], axis=0),
+        preferred_element_type=F32,
+    )
+
+
 def apply_kernel(distances, n_row, n_blocks, *refs):
     table_any, refs = refs[0], refs[1:]
     banks, refs = refs[: len(distances)], refs[len(distances) :]
@@ -171,8 +179,8 @@
                 odd = store(index, joined)
                 continue
             both = split(dot3(link, before[1]))
-            store(index - 1, before[0] - dot3(before[1], odd))
-            odd = store(index, joined + dot3(both, odd))
+            store(index - 1, before[0] - dot_deep(before[1], odd))
+            odd = store(index, joined + dot_deep(both, odd))
         if n_blocks % 2 and n_blocks > 1:
             free, link = work[-1]
             store(n_blocks - 1, free - dot3(link, odd))

time: 21.9 us -> 21.9 us (level)
  no operation moved by 1% of the time
where the time goes in v4:
time: 21.9 us; the launch traced here: 21.7 us
  starting transfers between devices  9.13 us (42%)
  waiting for transfers between devices  6.18 us (28%)
  Pallas kernels  3.92 us (18%)
  other arithmetic  1.08 us (5%)
  between operations  0.71 us (3%)
  local copies, waits for them, and re-layouts  0.67 us (3%)
    ppermute x10, starting transfers between devices, send(): return lax.ppermute(x, AXES, to)  9.13 us
    ppermute x10, waiting for transfers between devices, send(): return lax.ppermute(x, AXES, to)  6.18 us
    pallas_call x1, Pallas kernels, on_device(): pl.pallas_call(functools.partial(apply_kernel, [by for _, by in late], n_...  2.54 us
    pallas_call x1, Pallas kernels, on_device(): pl.pallas_call(functools.partial(unpack_kernel, [by for _, by in early]),...  1.18 us
    concatenate x1, other arithmetic, pack(): jnp.concatenate([factor.reshape(nb, 1, nb), jnp.transpose(vectors, (1, 0,...  1.08 us
    pad x1, local copies, waits for them, and re-layouts, on_device(): jnp.pad(plan, ((0, 7), (0, nb - n_blocks)), constant_values=offsets[0])  0.66 us
  transfers between devices with their start and end apart: 10, of which 3 were waited for; matrix products, arithmetic and copies ran while one was open for 8% of the time, Pallas kernels for 6%

profile of v4, /device:TPU:0, one launch (start us, length us, event | category | flops | bytes accessed | tf_op | source)
XLA Modules:
  0.0 21.7 jit_solution(2102283945094515924)
XLA Ops:
  0.0 0.0 copy-start
  0.0 3.0 %collective-permute-start.3 = (f32[256,128]{1,0:T(8,128)}, f32[256,128]{1,0:T(8,128)S(1)}, u32[]{:S(2)}, u32[]{:S(2)}) collective-permute-start(f32[256,128]{1,0:T(8,128)} %refs_2_.1), channel_id=1, source_target_pairs={{0,16},{1,17},{2,18},{3,19},{4,20},{5,21},{6,22},{7,23},{8,24},{9,... | collective-permute-start | bytes 393224 | tf_op jit(solution)/shard_map/ppermute | solution.py:239
  3.0 1.1 %pad_maximum_fusion.both_ref = f32[383,1,128]{2,1,0:T(1,128)S(1)} fusion(f32[255,1,128]{2,1,0:T(1,128)} %bitcast.4, f32[128,1,128]{2,1,0:T(1,128)} %bitcast.5), kind=kLoop, calls=%fused_computation | loop fusion | flops 49024 | bytes 392192 | tf_op jit(solution)/shard_map/concatenate | solution.py:36
  4.0 0.2 pack.1.refs_0_
  4.2 2.6 %collective-permute-start.7 = (f32[160,128]{1,0:T(8,128)S(1)}, f32[160,128]{1,0:T(8,128)S(1)}, u32[]{:S(2)}, u32[]{:S(2)}) collective-permute-start(f32[160,128]{1,0:T(8,128)S(1)} %pack.1.refs_0_), channel_id=1, source_target_pairs={{0,3},{1,2},{2,1},{3,0},{4,7},{5,6},{6,5},{7,4},{8,10},{9,11},{10,... | collective-permute-start | bytes 245768 | tf_op jit(solution)/shard_map/ppermute | solution.py:239
  6.8 2.5 %collective-permute-start.6 = (f32[160,128]{1,0:T(8,128)S(1)}, f32[160,128]{1,0:T(8,128)S(1)}, u32[]{:S(2)}, u32[]{:S(2)}) collective-permute-start(f32[160,128]{1,0:T(8,128)S(1)} %pack.1.refs_0_), channel_id=1, source_target_pairs={{0,6},{1,7},{2,4},{3,5},{4,2},{5,3},{6,0},{7,1},{8,13},{9,12},{10,... | collective-permute-start | bytes 245768 | tf_op jit(solution)/shard_map/ppermute | solution.py:239
  9.3 0.5 %collective-permute-start.5 = (f32[160,128]{1,0:T(8,128)S(1)}, f32[160,128]{1,0:T(8,128)S(1)}, u32[]{:S(2)}, u32[]{:S(2)}) collective-permute-start(f32[160,128]{1,0:T(8,128)S(1)} %pack.1.refs_0_), channel_id=1, source_target_pairs={{0,1},{1,0},{2,3},{3,2},{4,5},{5,4},{6,7},{7,6},{8,9},{9,8},{10,11... | collective-permute-start | bytes 245768 | tf_op jit(solution)/shard_map/ppermute | solution.py:239
  9.8 0.1 collective-permute-start
  9.9 0.0 collective-permute-done.7.refs_3_
  9.9 0.0 collective-permute-start.2
  9.9 0.0 collective-permute-done.3.refs_4_
  9.9 0.5 %collective-permute-start.4 = (f32[256,128]{1,0:T(8,128)S(1)}, f32[256,128]{1,0:T(8,128)S(1)}, u32[]{:S(2)}, u32[]{:S(2)}) collective-permute-start(f32[256,128]{1,0:T(8,128)S(1)} %collective-permute-done.3.refs_4_), channel_id=1, source_target_pairs={{0,8},{1,9},{2,10},{3,11},{4,12},{5,13},{6,14},{7,15},{8,0},{9,1},... | collective-permute-start | bytes 393224 | tf_op jit(solution)/shard_map/ppermute | solution.py:239
  10.4 2.7 %collective-permute-done.6.refs_2_ = f32[160,128]{1,0:T(8,128)S(1)} collective-permute-done((f32[160,128]{1,0:T(8,128)S(1)}, f32[160,128]{1,0:T(8,128)S(1)}, u32[]{:S(2)}, u32[]{:S(2)}) %collective-permute-start.6) | collective-permute-done | bytes 81952 | tf_op jit(solution)/shard_map/ppermute | solution.py:239
  13.1 0.0 collective-permute-start.9
  13.1 0.6 %collective-permute-done.5.refs_1_ = f32[160,128]{1,0:T(8,128)S(1)} collective-permute-done((f32[160,128]{1,0:T(8,128)S(1)}, f32[160,128]{1,0:T(8,128)S(1)}, u32[]{:S(2)}, u32[]{:S(2)}) %collective-permute-start.5) | collective-permute-done | bytes 81952 | tf_op jit(solution)/shard_map/ppermute | solution.py:239
  13.7 0.0 collective-permute-start.8
  13.7 2.9 %collective-permute-done.refs_4_ = f32[160,128]{1,0:T(8,128)S(1)} collective-permute-done((f32[160,128]{1,0:T(8,128)S(1)}, f32[160,128]{1,0:T(8,128)S(1)}, u32[]{:S(2)}, u32[]{:S(2)}) %collective-permute-start) | collective-permute-done | bytes 81952 | tf_op jit(solution)/shard_map/ppermute | solution.py:239
  16.6 0.0 collective-permute-start.1
  17.2 0.7 %pad.4.refs_0_ = s32[8,128]{1,0:T(8,128)S(1)} pad(s32[1,6]{1,0:T(1,128)} %param.7, s32[]{:T(128)} %bitcast.3), padding=0_7x0_122 | pad | bytes 4124 | tf_op jit(solution)/shard_map/jit(_pad)/pad | solution.py:252
  17.9 0.0 collective-permute-done.9.refs_6_
  17.9 0.0 collective-permute-done.8.refs_5_
  17.9 1.2 %unpack_early.1.refs_6_ = bf16[8,8,128,128]{3,2,1,0:T(8,128)(2,1)S(1)} custom-call(f32[160,128]{1,0:T(8,128)S(1)} %pack.1.refs_0_, f32[160,128]{1,0:T(8,128)S(1)} %collective-permute-done.5.refs_1_, f32[160,128]{1,0:T(8,128)S(1)} %collective-permute-done.6.refs_2_, f32[160,128]{1,0:T(8,128)S(1)} %collective-permute-done.7.refs_3_, ...), custom_call_target="tpu_custom_call" | custom-call | tf_op jit(solution)/shard_map/unpack_early/pallas_call | solution.py:258
  19.1 0.0 collective-permute-done.2.refs_3_
  19.1 0.0 collective-permute-done.1.refs_1_
  19.1 0.0 collective-permute-done.4.refs_5_
  19.1 0.0 copy-done
  19.1 2.5 %apply_blocks.1 = (f32[256,128]{1,0:T(8,128)}, bf16[8,8,128,128]{3,2,1,0:T(8,128)(2,1)S(1)}) custom-call(s32[8,128]{1,0:T(8,128)S(1)} %pad.4.refs_0_, f32[160,128]{1,0:T(8,128)S(1)} %collective-permute-done.1.refs_1_, f32[256,128]{1,0:T(8,128)S(1)} %copy-done, f32[256,128]{1,0:T(8,128)S(1)} %collective-permute-done.2.refs_3_, ...), custom_call_target="tpu_custom_call", output_to_operand_aliasing={{1}: (6, {})} | custom-call | tf_op jit(solution)/shard_map/apply_blocks/pallas_call | solution.py:267
Async XLA Ops:
  0.0 19.1 %copy-start = (f32[256,128]{1,0:T(8,128)S(1)}, f32[256,128]{1,0:T(8,128)}, u32[]{:S(2)}) copy-start(f32[256,128]{1,0:T(8,128)} %refs_2_.1) | copy-start | bytes 393220
  0.0 9.9 %collective-permute-start.3 = (f32[256,128]{1,0:T(8,128)}, f32[256,128]{1,0:T(8,128)S(1)}, u32[]{:S(2)}, u32[]{:S(2)}) collective-permute-start(f32[256,128]{1,0:T(8,128)} %refs_2_.1), channel_id=1, source_target_pairs={{0,16},{1,17},{2,18},{3,19},{4,20},{5,21},{6,22},{7,23},{8,24},{9,... | collective-permute-start | bytes 393224 | tf_op jit(solution)/shard_map/ppermute | solution.py:239
  4.2 5.7 %collective-permute-start.7 = (f32[160,128]{1,0:T(8,128)S(1)}, f32[160,128]{1,0:T(8,128)S(1)}, u32[]{:S(2)}, u32[]{:S(2)}) collective-permute-start(f32[160,128]{1,0:T(8,128)S(1)} %pack.1.refs_0_), channel_id=1, source_target_pairs={{0,3},{1,2},{2,1},{3,0},{4,7},{5,6},{6,5},{7,4},{8,10},{9,11},{10,... | collective-permute-start | bytes 245768 | tf_op jit(solution)/shard_map/ppermute | solution.py:239
  6.8 6.3 %collective-permute-start.6 = (f32[160,128]{1,0:T(8,128)S(1)}, f32[160,128]{1,0:T(8,128)S(1)}, u32[]{:S(2)}, u32[]{:S(2)}) collective-permute-start(f32[160,128]{1,0:T(8,128)S(1)} %pack.1.refs_0_), channel_id=1, source_target_pairs={{0,6},{1,7},{2,4},{3,5},{4,2},{5,3},{6,0},{7,1},{8,13},{9,12},{10,... | collective-permute-start | bytes 245768 | tf_op jit(solution)/shard_map/ppermute | solution.py:239
  9.3 4.4 %collective-permute-start.5 = (f32[160,128]{1,0:T(8,128)S(1)}, f32[160,128]{1,0:T(8,128)S(1)}, u32[]{:S(2)}, u32[]{:S(2)}) collective-permute-start(f32[160,128]{1,0:T(8,128)S(1)} %pack.1.refs_0_), channel_id=1, source_target_pairs={{0,1},{1,0},{2,3},{3,2},{4,5},{5,4},{6,7},{7,6},{8,9},{9,8},{10,11... | collective-permute-start | bytes 245768 | tf_op jit(solution)/shard_map/ppermute | solution.py:239
  9.8 6.8 %collective-permute-start = (f32[160,128]{1,0:T(8,128)S(1)}, f32[160,128]{1,0:T(8,128)S(1)}, u32[]{:S(2)}, u32[]{:S(2)}) collective-permute-start(f32[160,128]{1,0:T(8,128)S(1)} %pack.1.refs_0_), channel_id=1, source_target_pairs={{0,4},{1,5},{2,6},{3,7},{4,0},{5,1},{6,2},{7,3},{8,15},{9,14},{10,... | collective-permute-start | bytes 245768 | tf_op jit(solution)/shard_map/ppermute | solution.py:239
  9.9 9.2 %collective-permute-start.2 = (f32[256,128]{1,0:T(8,128)}, f32[256,128]{1,0:T(8,128)S(1)}, u32[]{:S(2)}, u32[]{:S(2)}) collective-permute-start(f32[256,128]{1,0:T(8,128)} %refs_2_.1), channel_id=1, source_target_pairs={{0,8},{1,9},{2,10},{3,11},{4,12},{5,13},{6,14},{7,15},{8,0},{9,1},... | collective-permute-start | bytes 393224 | tf_op jit(solution)/shard_map/ppermute | solution.py:239
  9.9 9.2 %collective-permute-start.4 = (f32[256,128]{1,0:T(8,128)S(1)}, f32[256,128]{1,0:T(8,128)S(1)}, u32[]{:S(2)}, u32[]{:S(2)}) collective-permute-start(f32[256,128]{1,0:T(8,128)S(1)} %collective-permute-done.3.refs_4_), channel_id=1, source_target_pairs={{0,8},{1,9},{2,10},{3,11},{4,12},{5,13},{6,14},{7,15},{8,0},{9,1},... | collective-permute-start | bytes 393224 | tf_op jit(solution)/shard_map/ppermute | solution.py:239
  13.1 4.8 %collective-permute-start.9 = (f32[160,128]{1,0:T(8,128)S(1)}, f32[160,128]{1,0:T(8,128)S(1)}, u32[]{:S(2)}, u32[]{:S(2)}) collective-permute-start(f32[160,128]{1,0:T(8,128)S(1)} %collective-permute-done.7.refs_3_), channel_id=1, source_target_pairs={{0,8},{1,9},{2,10},{3,11},{4,12},{5,13},{6,14},{7,15},{8,0},{9,1},... | collective-permute-start | bytes 245768 | tf_op jit(solution)/shard_map/ppermute | solution.py:239
  13.7 4.2 %collective-permute-start.8 = (f32[160,128]{1,0:T(8,128)S(1)}, f32[160,128]{1,0:T(8,128)S(1)}, u32[]{:S(2)}, u32[]{:S(2)}) collective-permute-start(f32[160,128]{1,0:T(8,128)S(1)} %collective-permute-done.6.refs_2_), channel_id=1, source_target_pairs={{0,8},{1,9},{2,10},{3,11},{4,12},{5,13},{6,14},{7,15},{8,0},{9,1},... | collective-permute-start | bytes 245768 | tf_op jit(solution)/shard_map/ppermute | solution.py:239
  16.6 2.5 %collective-permute-start.1 = (f32[160,128]{1,0:T(8,128)S(1)}, f32[160,128]{1,0:T(8,128)S(1)}, u32[]{:S(2)}, u32[]{:S(2)}) collective-permute-start(f32[160,128]{1,0:T(8,128)S(1)} %collective-permute-done.refs_4_), channel_id=1, source_target_pairs={{0,8},{1,9},{2,10},{3,11},{4,12},{5,13},{6,14},{7,15},{8,0},{9,1},... | collective-permute-start | bytes 245768 | tf_op jit(solution)/shard_map/ppermute | solution.py:239
